TPU v7x, 32 devices: a whole 2x2x4 slice. The times are simulated.
32 devices in a mesh: dp: 8 (over z, x), tensor: 4 (over y, core).
Axes of the slice: x: 2, y: 2, z: 4, core: 2. Of those that a mesh axis runs over, the one named last changes fastest.
Arguments:
- frames: bfloat16 [16, 800, 768], P('dp', 'tensor'), may hold values from -6 to 6
- cotangent: float32 [16, 800, 768], P('dp', 'tensor'), may hold values from -6 to 6
- lengths: int32 [16], P('dp'), may hold values from 100 to 780
- query_weight: bfloat16 [768, 768], P(None, 'tensor'), may hold values from -0.21875 to 0.21875
- query_bias: float32 [768], P('tensor'), may hold values from -3 to 3
- key_weight: bfloat16 [768, 768], P(None, 'tensor'), may hold values from -0.21875 to 0.21875
- value_weight: bfloat16 [768, 768], P(None, 'tensor'), may hold values from -0.21875 to 0.21875
- value_bias: float32 [768], P('tensor'), may hold values from -3 to 3
- out_weight: bfloat16 [768, 768], P('tensor'), may hold values from -1.75 to 1.75
- out_bias: float32 [768], replicated, may hold values from -3 to 3
- first_gain: float32 [768], replicated, may hold values from 0.5 to 1.5
- first_shift: float32 [768], replicated, may hold values from -3 to 3
- up_weight: bfloat16 [768, 3072], P(None, 'tensor'), may hold values from -0.21875 to 0.21875
- up_bias: float32 [3072], P('tensor'), may hold values from -3 to 3
- down_weight: bfloat16 [3072, 768], P('tensor'), may hold values from -0.109375 to 0.109375
- down_bias: float32 [768], replicated, may hold values from -3 to 3
- second_gain: float32 [768], replicated, may hold values from 0.5 to 1.5
- second_shift: float32 [768], replicated, may hold values from -3 to 3
Outputs:
- layer_output: bfloat16 [16, 800, 768], P('dp', 'tensor')
- input_gradient: float32 [16, 800, 768], P('dp', 'tensor')
- query_weight_gradient: float32 [768, 768], P(None, 'tensor')
- query_bias_gradient: float32 [768], P('tensor')
- key_weight_gradient: float32 [768, 768], P(None, 'tensor')
- value_weight_gradient: float32 [768, 768], P(None, 'tensor')
- value_bias_gradient: float32 [768], P('tensor')
- out_weight_gradient: float32 [768, 768], P('tensor')
- out_bias_gradient: float32 [768], replicated
- first_gain_gradient: float32 [768], replicated
- first_shift_gradient: float32 [768], replicated
- up_weight_gradient: float32 [768, 3072], P(None, 'tensor')
- up_bias_gradient: float32 [3072], P('tensor')
- down_weight_gradient: float32 [3072, 768], P('tensor')
- down_bias_gradient: float32 [768], replicated
- second_gain_gradient: float32 [768], replicated
- second_shift_gradient: float32 [768], replicated
All inputs are finite; a program needn't handle non-finite values.
Results may differ from a plain program's by a relative error of at most 0.019.
Values may be sent and summed in bfloat16 or wider, within the bound.
A program may use at most 192 MiB of HBM per device.

v0:
```python
import functools
import types

import jax
import jax.numpy as jnp
from jax import lax
from jax.experimental import pallas as pl
from jax.experimental.pallas import tpu as pltpu
from jax.sharding import PartitionSpec as P

MESH = pl.DeviceIdType.MESH
HEAD_DIM = 64
EPSILON = 1e-05
ROOT_HALF = 0.7071067811865476
INVERSE_ROOT_TAU = 0.3989422804014327
MASKED = -1e30
VMEM_BYTES = 62 << 20
POLLS = (4, 2, 1, 2, 2, 1)
BF = jnp.bfloat16
F32 = jnp.float32


def up_to(size, unit):
    return (size + unit - 1) // unit * unit


def dot(left, right):
    return jnp.dot(left, right, preferred_element_type=F32)


def dot_nt(left, right):
    return lax.dot_general(left, right, (((1,), (1,)), ((), ())), preferred_element_type=F32)


def dot_tn(left, right):
    return lax.dot_general(left, right, (((0,), (0,)), ((), ())), preferred_element_type=F32)


def pad_rows(rows, size):
    extra = size - rows.shape[0]
    if extra == 0:
        return rows
    return jnp.concatenate([rows, jnp.zeros((extra, rows.shape[1]), rows.dtype)], axis=0)


class Group:
    def __init__(self):
        self.dp = lax.axis_index("dp")
        self.own = lax.axis_index("tensor")
        self.y = self.own // 2
        self.core = self.own % 2
        self.mate = self.y * 2 + (1 - self.core)
        self.far = (1 - self.y) * 2 + self.core

    def greet(self, dp_peers):
        barrier = pltpu.get_barrier_semaphore()
        peers = [(self.dp, self.mate), (self.dp, self.far)] + [(peer, self.own) for peer in dp_peers]
        for peer in peers:
            pl.semaphore_signal(barrier, inc=1, device_id=peer, device_id_type=MESH)
        return lambda: pl.semaphore_wait(barrier, len(peers))

    def share(self, turn):
        late = turn // 2
        other = ((turn + 1) // 2) % 2
        ybit = (1 - self.y) * (1 - late) + self.y * late
        core = self.core * (1 - other) + (1 - self.core) * other
        return ybit * 2 + core

    def copy(self, source, target, send, recv, peer):
        return pltpu.make_async_remote_copy(
            src_ref=source,
            dst_ref=target,
            send_sem=send,
            recv_sem=recv,
            device_id=(self.dp, peer),
            device_id_type=MESH,
        )


class Gather:
    def __init__(self, group, full, send, recv):
        self.group, self.full, self.send, self.recv = group, full, send, recv

    def _copy(self, seq, kind):
        group = self.group
        share = group.far if kind == 2 else group.own
        slot = self.full.at[seq, share]
        peer = group.far if kind == 0 else group.mate
        return group.copy(slot, slot, self.send.at[seq, kind], self.recv.at[seq, kind], peer)

    def start(self, seq):
        self._copy(seq, 0).start()
        self._copy(seq, 1).start()

    def wait(self, seq, turn):
        @pl.when(turn == 0)
        def _():
            self._copy(seq, 0).wait_recv()
            self._copy(seq, 2).start()

        @pl.when(turn == 1)
        def _():
            self._copy(seq, 2).wait_recv()

        @pl.when(turn == 2)
        def _():
            self._copy(seq, 1).wait_recv()

    def close(self, seq):
        for kind in range(3):
            self._copy(seq, kind).wait_send()


class Scatter:
    def __init__(self, group, buffers, send, recv):
        self.group = group
        self.outgoing, self.keep, self.near, self.cross, self.landed = buffers
        self.send, self.recv = send, recv

    def _near(self, seq, index):
        return self.group.copy(
            self.outgoing.at[seq, index],
            self.near.at[seq, index],
            self.send.at[seq, index],
            self.recv.at[seq, index],
            self.group.mate,
        )

    def _cross(self, seq):
        return self.group.copy(
            self.cross.at[seq],
            self.landed.at[seq],
            self.send.at[seq, 2],
            self.recv.at[seq, 2],
            self.group.far,
        )

    def put(self, seq, turn, terms):
        @pl.when((turn == 0) | (turn == 3))
        def _():
            self.keep[seq, turn // 3] = terms

        @pl.when((turn == 1) | (turn == 2))
        def _():
            self.outgoing[seq, turn - 1] = terms.astype(BF)
            self._near(seq, turn - 1).start()

        @pl.when(turn == 2)
        def _():
            self._near(seq, 0).wait_recv()
            total = self.keep[seq, 0] + self.near[seq, 0].astype(F32)
            self.cross[seq] = total.astype(BF)
            self._cross(seq).start()

    def take(self, seq):
        self._near(seq, 1).wait_recv()
        self._cross(seq).wait_recv()
        for index in range(2):
            self._near(seq, index).wait_send()
        self._cross(seq).wait_send()
        return (
            self.keep[seq, 1]
            + self.near[seq, 1].astype(F32)
            + self.landed[seq].astype(F32)
        )


def norm(rows):
    centred = rows - jnp.mean(rows, axis=-1, keepdims=True)
    inverse = lax.rsqrt(jnp.mean(centred * centred, axis=-1, keepdims=True) + EPSILON)
    return centred * inverse, inverse


def norm_back(grad, normed, inverse, gain):
    scaled = grad * gain
    return inverse * (
        scaled
        - jnp.mean(scaled, axis=-1, keepdims=True)
        - normed * jnp.mean(scaled * normed, axis=-1, keepdims=True)
    )


def sum_rows(rows):
    return jnp.sum(rows, axis=0, keepdims=True)


def lane_index(rows, lanes):
    return lax.broadcasted_iota(jnp.int32, (rows, lanes), 1)


class Ring:
    def __init__(self, group, count, own, opening, landed, shared, sems, first, rows):
        self.group, self.count, self.steps = group, count, count - 1
        self.own, self.opening, self.landed, self.shared = own, opening, landed, shared
        self.add_send, self.add_recv, self.share_send, self.share_recv = sems
        self.half = own.shape[0] // (2 * count)
        self.first, self.rows = first, rows
        self.span = pl.ds(first, rows)
        self.place, self.right, self.left = ring_peers(group.dp, count)

    def _own(self, way, step):
        shift = self.count - 1 - step if way == 0 else 1 + step
        chunk = (self.place + shift) % self.count
        start = pl.multiple_of((2 * chunk + way) * self.half + self.first, 16)
        return self.own[pl.ds(start, self.rows)]

    def _copy(self, source, target, send, recv, way):
        return pltpu.make_async_remote_copy(
            src_ref=source,
            dst_ref=target,
            send_sem=send,
            recv_sem=recv,
            device_id=(self.right if way == 0 else self.left, self.group.own),
            device_id_type=MESH,
        )

    def _add(self, way, step, source=None):
        target = self.landed.at[way, step, self.span]
        return self._copy(
            target if source is None else source,
            target,
            self.add_send.at[way, step],
            self.add_recv.at[way, step],
            way,
        )

    def _share(self, way, step):
        shift = self.count - step if way == 0 else step
        slot = self.shared.at[(self.place + shift) % self.count, way, self.span]
        return self._copy(
            slot, slot, self.share_send.at[way, step], self.share_recv.at[way, step], way
        )

    def open(self):
        for way in range(2):
            self.opening[way, self.span] = self._own(way, 0).astype(BF)
            self._add(way, 0, self.opening.at[way, self.span]).start()

    def advance(self, step):
        last = self.steps - 1
        for way in range(2):
            if step < self.steps:
                self._add(way, step).wait_recv()
                total = self.landed[way, step, self.span].astype(F32) + self._own(way, step + 1)
                if step < last:
                    self.landed[way, step, self.span] = total.astype(BF)
                    self._add(way, step + 1, self.landed.at[way, step, self.span]).start()
                else:
                    self.shared[self.place, way, self.span] = total.astype(BF)
                    self._share(way, 0).start()
            else:
                turn = step - self.steps
                self._share(way, turn).wait_recv()
                if turn < last:
                    self._share(way, turn + 1).start()

    def close(self):
        for way in range(2):
            for step in range(self.steps):
                self._add(way, step).wait_send()
                self._share(way, step).wait_send()


def ring_peers(index, count):
    odd = index % 2
    place = (1 - odd) * (index // 2) + odd * (count - 1 - index // 2)

    def at(spot):
        late = spot // (count // 2)
        return (1 - late) * 2 * spot + late * (2 * (count - 1 - spot) + 1)

    return place, at((place + 1) % count), at((place + count - 1) % count)


def halving_peers(index, count):
    peers = []
    bit = 1
    while bit < count:
        peers.append(index + bit * (1 - 2 * ((index // bit) % 2)))
        bit *= 2
    return peers


class Totals:
    def __init__(self, group, peers, outgoing, arriving, send, recv, shared):
        self.group, self.shared = group, shared
        self.outgoing, self.arriving, self.send, self.recv = outgoing, arriving, send, recv
        own = group.own
        self.peers = [(group.dp, group.mate), (group.dp, group.far)] + [(peer, own) for peer in peers]

    def _copy(self, level):
        return pltpu.make_async_remote_copy(
            src_ref=self.outgoing.at[level],
            dst_ref=self.arriving.at[level],
            send_sem=self.send.at[level],
            recv_sem=self.recv.at[level],
            device_id=self.peers[level],
            device_id_type=MESH,
        )

    def begin(self, level, rows):
        self.outgoing[level] = rows
        self._copy(level).start()

    def end(self, level):
        self._copy(level).wait()
        other = self.arriving[level]
        if level < 2:
            place = lax.broadcasted_iota(jnp.int32, other.shape, 0)
            other = jnp.where(place < self.shared, other, 0.0)
        return self.outgoing[level] + other


def layer(count, names, *refs):
    r = types.SimpleNamespace(**dict(zip(names, refs)))
    seqs, share_rows, width = r.frames.shape
    rows = r.full_frames.shape[2]
    length = 4 * rows
    heads_width = r.query_weight.shape[0]
    lanes = r.wide_weight.shape[0] // 3
    heads = heads_width // HEAD_DIM
    group = Group()
    pairs = []
    ring_sides = []
    if count:
        pairs = halving_peers(group.dp, count)
        ring_sides = list(ring_peers(group.dp, count)[1:])
    met = group.greet(ring_sides + pairs)

    out_bias, first_gain, first_shift, down_bias, second_gain, second_shift, up_bias = (
        row[...].reshape(1, row.shape[0])
        for row in (
            r.out_bias, r.first_gain, r.first_shift, r.down_bias, r.second_gain, r.second_shift, r.up_bias,
        )
    )
    buffers = (r.outgoing, r.keep, r.near, r.cross, r.landed)
    gathers = [
        Gather(group, full, r.gather_send.at[index], r.gather_recv.at[index])
        for index, full in enumerate((r.full_frames, r.first_full, r.grad_mixed, r.grad_full))
    ]
    scatters = [
        Scatter(group, buffers, r.scatter_send.at[index], r.scatter_recv.at[index])
        for index in range(4)
    ]
    grad_total = r.hidden.at[0]
    heads_grad = r.hidden.at[1, pl.ds(0, 4 * heads_width)]
    grad_projected = r.activated.at[0]

    def each(stage):
        def body(seq, carry):
            stage(seq)
            return carry

        lax.fori_loop(0, seqs, body, 0)

    def turns(step):
        def body(turn, carry):
            step(turn)
            return carry

        lax.fori_loop(0, 4, body, 0)

    def at_share(share):
        return pl.ds(pl.multiple_of(share * rows, 16), rows)

    def place_frames(seq):
        r.full_frames[seq, group.own] = pad_rows(r.frames[seq].astype(F32), rows).astype(BF)

    each(place_frames)
    met()
    each(gathers[0].start)
    r.wide_weight[...] = jnp.zeros_like(r.wide_weight)
    for index, weight in enumerate((r.query_weight, r.key_weight, r.value_weight)):
        r.wide_weight[index * lanes : index * lanes + heads_width] = weight[...]
    r.wide_out[...] = jnp.zeros_like(r.wide_out)
    r.wide_out[:heads_width] = r.out_weight[...]
    r.projection_bias[...] = jnp.where(
        lane_index(1, 3 * lanes) == heads_width, HEAD_DIM**0.5, 0.0
    )
    r.projection_bias[:, :heads_width] = r.query_bias[...].reshape(1, heads_width)
    r.projection_bias[:, 2 * lanes : 2 * lanes + heads_width] = r.value_bias[...].reshape(1, heads_width)
    r.rows_sum[...] = jnp.zeros_like(r.rows_sum)

    def attention(seq):
        def project(step):
            turn = (1 - step // 2) * (3 - step) + (step // 2) * (step - 2)
            gathers[0].wait(seq, turn)
            share = group.share(turn)
            result = dot_nt(r.full_frames[seq, share], r.wide_weight[...]) + r.projection_bias[...]
            place = lax.broadcasted_iota(jnp.int32, (rows, lanes), 0)
            dead = (place >= share_rows) | (place + share * share_rows >= r.lengths[seq])
            flag = jnp.where(dead & (lane_index(rows, lanes) == heads_width), MASKED, 0.0)
            r.projected[seq, at_share(share), 0:lanes] = (
                result[:, :lanes].astype(BF) * HEAD_DIM ** (-0.5)
            ).astype(BF)
            r.projected[seq, at_share(share), lanes : 2 * lanes] = (
                result[:, lanes : 2 * lanes] + flag
            ).astype(BF)
            r.projected[seq, at_share(share), 2 * lanes : 3 * lanes] = result[:, 2 * lanes :].astype(BF)

        turns(project)

        def attend(block, carry):
            chip = (1 - group.y) * (1 - block) + group.y * block
            span = pl.ds(pl.multiple_of(chip * 2 * rows, 16), 2 * rows)
            queries = r.projected[seq, span, 0:lanes]
            lane = lane_index(2 * rows, lanes)
            mixed = jnp.zeros((2 * rows, lanes), F32)
            for head in range(heads):
                inside = lane // HEAD_DIM == head
                picked = jnp.where(inside | (lane == heads_width), queries, jnp.zeros_like(queries))
                scores = dot_nt(picked, r.projected[seq, :, lanes : 2 * lanes])
                top = jnp.max(scores, axis=-1, keepdims=True)
                exponent = jnp.exp(scores - top)
                weight = jnp.sum(exponent, axis=-1, keepdims=True)
                r.log_total[seq, chip, head : head + 1] = jnp.transpose(top + jnp.log(weight))
                part = dot(exponent.astype(BF), r.projected[seq, :, 2 * lanes : 3 * lanes])
                mixed = jnp.where(inside, part * (1.0 / weight), mixed)
            r.context[seq, span] = mixed.astype(BF)
            for half in range(2):
                turn = 2 * block + half
                mixed = r.context[seq, at_share(group.share(turn))]
                scatters[0].put(seq, turn, dot(mixed, r.wide_out[...]))
            return carry

        lax.fori_loop(0, 2, attend, 0)

    each(attention)

    def first_norm(seq):
        attended = scatters[0].take(seq)
        normed, inverse = norm(r.full_frames[seq, group.own].astype(F32) + attended + out_bias)
        r.first_normed[seq] = normed
        r.first_inverse[seq] = inverse
        r.first_full[seq, group.own] = (normed * first_gain + first_shift).astype(BF)
        gathers[1].start(seq)

    each(first_norm)

    def feed(seq):
        def step(turn):
            gathers[1].wait(seq, turn)
            share = group.share(turn)
            inner = dot(r.first_full[seq, share], r.up_weight[...]) + up_bias
            r.hidden[seq, at_share(share)] = inner
            active = (0.5 * inner * (1.0 + lax.erf(inner * ROOT_HALF))).astype(BF)
            r.activated[seq, at_share(share)] = active
            scatters[1].put(seq, turn, dot(active, r.down_weight[...]))

        turns(step)

    each(feed)

    def second_norm(seq):
        mixed = scatters[1].take(seq)
        first = r.first_normed[seq] * first_gain + first_shift
        normed, inverse = norm(first + mixed + down_bias)
        place = lax.broadcasted_iota(jnp.int32, (rows, width), 0)
        live = (place < share_rows) & (place + group.own * share_rows < r.lengths[seq])
        grad = jnp.where(live, pad_rows(r.cotangent[seq], rows), 0.0)
        back = norm_back(grad, normed, inverse, second_gain)
        r.grad_mixed[seq, group.own] = back.astype(BF)
        gathers[2].start(seq)
        r.grad_rows[seq] = back
        r.layer_output[seq] = (normed * second_gain + second_shift)[:share_rows].astype(BF)
        r.rows_sum[0:1] += sum_rows(grad * normed)
        r.rows_sum[1:2] += sum_rows(grad)
        r.rows_sum[2:3] += sum_rows(back)

    each(second_norm)

    def feed_back(seq):
        def step(turn):
            gathers[2].wait(seq, turn)
            share = group.share(turn)
            grad_active = dot_nt(r.grad_mixed[seq, share], r.down_weight[...])
            inner = r.hidden[seq, at_share(share)]
            slope = (
                0.5 * (1.0 + lax.erf(inner * ROOT_HALF))
                + inner * jnp.exp(-0.5 * inner * inner) * INVERSE_ROOT_TAU
            )
            grad = (grad_active * slope).astype(BF)
            r.grad_hidden[seq, at_share(share)] = grad
            r.rows_sum[6:7] += sum_rows(grad.astype(F32))
            scatters[2].put(seq, turn, dot_nt(grad, r.up_weight[...]))

        turns(step)

    each(feed_back)

    def feed_weights(seq):
        down = dot_tn(r.activated[seq], r.grad_mixed[seq].reshape(length, width))
        r.down_grad[...] = down if seq == 0 else r.down_grad[...] + down
        up = dot_tn(r.first_full[seq].reshape(length, width), r.grad_hidden[seq])
        r.up_grad[...] = up if seq == 0 else r.up_grad[...] + up

    def first_back(seq):
        grad = r.grad_rows[seq] + scatters[2].take(seq)
        normed = r.first_normed[seq]
        back = norm_back(grad, normed, r.first_inverse[seq], first_gain)
        r.grad_full[seq, group.own] = back.astype(BF)
        gathers[3].start(seq)
        r.grad_rows[seq] = back
        r.rows_sum[3:4] += sum_rows(grad * normed)
        r.rows_sum[4:5] += sum_rows(grad)
        r.rows_sum[5:6] += sum_rows(back)

    queue = []

    def advance_both(both, step):
        for ring in both:
            ring.advance(step)

    def poll(times=1):
        for _ in range(times):
            if queue:
                queue.pop(0)()

    for seq in range(seqs):
        feed_weights(seq)
        if seq == seqs - 1 and count:
            half = width // (2 * count)

            def make_ring(index, own, first, size):
                return Ring(
                    group,
                    count,
                    own,
                    r.opening.at[index],
                    r.ring_landed.at[index],
                    r.ring_shared.at[index],
                    [
                        sem.at[index, first // 16]
                        for sem in (r.add_send, r.add_recv, r.share_send, r.share_recv)
                    ],
                    first,
                    size,
                )

            rings = [
                make_ring(index, own, first, 16)
                for first in range(0, half, 16)
                for index, own in enumerate((r.up_grad, r.down_grad))
            ]
            late_rings = [make_ring(2, heads_grad, first, 16) for first in range(0, half, 16)]
            for ring in rings:
                ring.open()
            for step in range(2 * (count - 1)):
                for first in range(0, len(rings), 2):
                    queue.append(functools.partial(advance_both, rings[first : first + 2], step))
        first_back(seq)
    poll(POLLS[0])
    if count:
        totals = Totals(
            group, pairs, r.small_out, r.small_in, r.small_send, r.small_recv, 6
        )
        totals.begin(0, r.rows_sum[...])
    heads_grad[...] = jnp.zeros_like(heads_grad)

    def store_input(seq):
        r.input_grad[seq] = (scatters[3].take(seq) + r.grad_rows[seq])[:share_rows]

    for seq in range(seqs):

        def step(turn):
            gathers[3].wait(seq, turn)
            share = group.share(turn)
            r.grad_context[at_share(share)] = dot_nt(r.grad_full[seq, share], r.wide_out[...]).astype(BF)
            heads_grad[3 * heads_width :] += dot_tn(
                r.context[seq, at_share(share)], r.grad_full[seq, share]
            )[:heads_width]

        turns(step)
        poll(POLLS[1])
        grad_total[...] = jnp.zeros_like(grad_total)
        keys = r.projected[seq, :, lanes : 2 * lanes]
        lane = lane_index(length, lanes)
        key_columns = jnp.transpose(keys.astype(F32) * HEAD_DIM ** (-0.5)).astype(BF)
        for head in range(heads):
            inside = lane // HEAD_DIM == head
            queries = r.projected[seq, :, 0:lanes]
            picked = jnp.where(inside | (lane == heads_width), queries, jnp.zeros_like(queries))
            row = jnp.concatenate(
                [r.log_total[seq, chip, head : head + 1] for chip in range(2)], axis=1
            )
            weights = jnp.exp(dot_nt(keys, picked) - row)
            grads = r.grad_context[...]
            part = dot(weights.astype(BF), grads)
            span = slice(2 * lanes, 3 * lanes)
            grad_total[:, span] = jnp.where(inside, part, grad_total[:, span])
            poll(POLLS[2])
            slopes = weights * dot_nt(
                r.projected[seq, :, 2 * lanes : 3 * lanes],
                jnp.where(inside, grads, jnp.zeros_like(grads)),
            )
            slopes = (slopes - weights * jnp.sum(slopes, axis=0, keepdims=True)).astype(BF)
            part = dot(slopes, queries)
            span = slice(lanes, 2 * lanes)
            grad_total[:, span] = jnp.where(inside, part, grad_total[:, span])
            span = slice(head * HEAD_DIM, (head + 1) * HEAD_DIM)
            grad_total[:, span] = jnp.transpose(dot(key_columns[span], slopes))
            poll(POLLS[3])

        def finish(turn):
            share = group.share(turn)
            grads = grad_total[at_share(share)].astype(BF)
            grad_projected[at_share(share)] = grads
            r.rows_sum[7:8] += sum_rows(grads.astype(F32))
            scatters[3].put(seq, turn, dot(grads, r.wide_weight[...]))

        turns(finish)
        poll(POLLS[4])
        for index in range(3):
            heads_grad[index * heads_width : (index + 1) * heads_width] += dot_tn(
                grad_projected[:, index * lanes : (index + 1) * lanes],
                r.full_frames[seq].reshape(length, width),
            )[:heads_width]
        poll(POLLS[5])
        if seq == 0:
            if count:
                totals.begin(1, totals.end(0))
        else:
            store_input(seq - 1)

    if count:
        for ring in late_rings:
            ring.open()
        place = lax.broadcasted_iota(jnp.int32, r.rows_sum.shape, 0)
        totals.begin(2, jnp.where(place == 7, r.rows_sum[...], totals.end(1)))
        copies = [
            pltpu.make_async_copy(r.ring_shared.at[index], out, r.out_sem.at[index])
            for index, out in enumerate((r.up_sum, r.down_sum, r.heads_sum))
        ]
        level = 2
        last = len(pairs) + 1
        for step in range(2 * (count - 1)):
            for ring in late_rings:
                ring.advance(step)
                poll()
            if step == 2:
                store_input(seqs - 1)
            if step % 3 == 2 and level <= last:
                rows_total = totals.end(level)
                level += 1
                if level <= last:
                    totals.begin(level, rows_total)
                else:
                    r.sums[...] = rows_total
        poll(len(queue))
        for copy in copies:
            copy.start()
        for ring in rings + late_rings:
            ring.close()
    else:
        store_input(seqs - 1)
        r.sums[...] = r.rows_sum[...]
        copies = [
            pltpu.make_async_copy(own, out, r.out_sem.at[index])
            for index, (own, out) in enumerate(
                ((r.up_grad, r.up_sum), (r.down_grad, r.down_sum), (heads_grad, r.heads_sum))
            )
        ]
        for copy in copies:
            copy.start()
    for seq in range(seqs):
        for gather in gathers:
            gather.close(seq)
    for copy in copies:
        copy.wait()


VMEM_SPEC = pl.BlockSpec(memory_space=pltpu.VMEM)
ANY_SPEC = pl.BlockSpec(memory_space=pl.ANY)


def widen(columns, refs, *rest):
    r = types.SimpleNamespace(**dict(zip(refs, rest)))
    heads_width = r.query_bias.shape[0]
    width = r.up.shape[1]
    plain = [
        (r.layer_in, r.layer_stage, r.layer_output),
        (r.input_in, r.input_stage, r.input_grad),
    ]
    plain_loads = [
        pltpu.make_async_copy(source, stage, r.plain_sem.at[index])
        for index, (source, stage, _) in enumerate(plain)
    ]
    loads = [
        pltpu.make_async_copy(source, r.narrow.at[index], r.load_sem.at[index])
        for index, source in enumerate((r.up_in, r.down_in, r.heads_in))
    ]
    for copy in loads + plain_loads:
        copy.start()
    stores = []
    for index, load in enumerate(loads):
        load.wait()
        r.wide[index] = r.narrow[index].astype(F32).reshape(width, width)
        if index < 2:
            parts = [(r.wide.at[index], (r.up, r.down)[index])]
        else:
            parts = [
                (r.wide.at[index, pl.ds(part * heads_width, heads_width)], target)
                for part, target in enumerate((r.query, r.key, r.value, r.out))
            ]
        for source, target in parts:
            store = pltpu.make_async_copy(source, target, r.store_sem.at[len(stores)])
            store.start()
            stores.append(store)
    for load, (_, stage, target) in zip(plain_loads, plain):
        load.wait()
        store = pltpu.make_async_copy(stage, target, r.store_sem.at[len(stores)])
        store.start()
        stores.append(store)
    rows = (
        r.second_gain, r.second_shift, r.down_bias, r.first_gain, r.first_shift, r.out_bias, r.up_bias,
    )
    for index, row in enumerate(rows):
        row[...] = r.sums[index]
    r.query_bias[...] = r.sums[7, 0:heads_width]
    r.value_bias[...] = r.sums[7, columns : columns + heads_width]
    for copy in stores:
        copy.wait()


def shards(
    frames,
    cotangent,
    lengths,
    query_weight,
    query_bias,
    key_weight,
    value_weight,
    value_bias,
    out_weight,
    out_bias,
    first_gain,
    first_shift,
    up_weight,
    up_bias,
    down_weight,
    down_bias,
    second_gain,
    second_shift,
):
    seqs, share_rows, width = frames.shape
    rows = up_to(share_rows, 16)
    length = 4 * rows
    heads_width = query_weight.shape[1]
    inner = up_weight.shape[1]
    lanes = up_to(heads_width + 1, 128)
    shape = jax.ShapeDtypeStruct
    count = lax.axis_size("dp")
    ringed = count & (count - 1) == 0 and width % (32 * count) == 0
    half = width // (2 * count)
    levels = 2 + count.bit_length() - 1
    full = pltpu.VMEM((seqs, 4, rows, width), BF)
    part = pltpu.VMEM((seqs, rows, width), BF)
    stream = pltpu.VMEM((seqs, rows, width), F32)
    inputs = dict(
        lengths=lengths,
        frames=frames,
        cotangent=cotangent,
        query_weight=query_weight.T,
        query_bias=query_bias,
        key_weight=key_weight.T,
        value_weight=value_weight.T,
        value_bias=value_bias,
        out_weight=out_weight,
        out_bias=out_bias,
        first_gain=first_gain,
        first_shift=first_shift,
        up_weight=up_weight,
        up_bias=up_bias,
        down_weight=down_weight,
        down_bias=down_bias,
        second_gain=second_gain,
        second_shift=second_shift,
    )
    summed = (
        shape((count, 2, half, width), BF) if ringed else shape((width, width), F32)
    )
    outputs = dict(
        layer_output=shape(frames.shape, BF),
        input_grad=shape(frames.shape, F32),
        sums=shape((8, width), F32),
        up_sum=summed,
        down_sum=summed,
        heads_sum=summed,
    )
    scratch = dict(
        wide_weight=pltpu.VMEM((3 * lanes, width), BF),
        wide_out=pltpu.VMEM((lanes, width), BF),
        projection_bias=pltpu.VMEM((1, 3 * lanes), F32),
        rows_sum=pltpu.VMEM((8, width), F32),
        full_frames=full,
        first_full=full,
        grad_mixed=full,
        grad_full=full,
        projected=pltpu.VMEM((seqs, length, 3 * lanes), BF),
        context=pltpu.VMEM((seqs, length, lanes), BF),
        log_total=pltpu.VMEM((seqs, 2, 8, 2 * rows), F32),
        first_normed=stream,
        first_inverse=pltpu.VMEM((seqs, rows, 1), F32),
        grad_rows=stream,
        hidden=pltpu.VMEM((seqs, length, inner), F32),
        activated=pltpu.VMEM((seqs, length, inner), BF),
        grad_hidden=pltpu.VMEM((seqs, length, inner), BF),
        grad_context=pltpu.VMEM((length, lanes), BF),
        up_grad=pltpu.VMEM(up_weight.shape, F32),
        down_grad=pltpu.VMEM(down_weight.shape, F32),
        outgoing=pltpu.VMEM((seqs, 2, rows, width), BF),
        keep=pltpu.VMEM((seqs, 2, rows, width), F32),
        near=pltpu.VMEM((seqs, 2, rows, width), BF),
        cross=part,
        landed=part,
        gather_send=pltpu.SemaphoreType.DMA((4, seqs, 3)),
        gather_recv=pltpu.SemaphoreType.DMA((4, seqs, 3)),
        scatter_send=pltpu.SemaphoreType.DMA((4, seqs, 3)),
        scatter_recv=pltpu.SemaphoreType.DMA((4, seqs, 3)),
        out_sem=pltpu.SemaphoreType.DMA((3,)),
    )
    if ringed:
        ring_sem = pltpu.SemaphoreType.DMA((3, half // 16, 2, count - 1))
        scratch.update(
            opening=pltpu.VMEM((3, 2, half, width), BF),
            ring_landed=pltpu.VMEM((3, 2, count - 1, half, width), BF),
            ring_shared=pltpu.VMEM((3, count, 2, half, width), BF),
            add_send=ring_sem,
            add_recv=ring_sem,
            share_send=ring_sem,
            share_recv=ring_sem,
            small_out=pltpu.VMEM((levels, 8, width), F32),
            small_in=pltpu.VMEM((levels, 8, width), F32),
            small_send=pltpu.SemaphoreType.DMA((levels,)),
            small_recv=pltpu.SemaphoreType.DMA((levels,)),
        )
    outs = pl.pallas_call(
        functools.partial(layer, count if ringed else 0, [*inputs, *outputs, *scratch]),
        out_shape=list(outputs.values()),
        in_specs=[pl.BlockSpec(memory_space=pltpu.SMEM)] + [VMEM_SPEC] * (len(inputs) - 1),
        out_specs=[VMEM_SPEC] * 3 + [ANY_SPEC] * 3,
        scratch_shapes=list(scratch.values()),
        compiler_params=pltpu.CompilerParams(
            collective_id=0, has_side_effects=True, vmem_limit_bytes=VMEM_BYTES
        ),
        name="layer",
    )(*inputs.values())
    layer_output, input_grad, sums = outs[:3]
    if not ringed:
        up_grad, down_grad, heads_grad = lax.psum(tuple(outs[3:]), "dp")
        sums = lax.psum(sums, "dp")
        sums = jnp.concatenate([lax.psum(sums[:6], "tensor"), sums[6:]])
        parts = [heads_grad[index * heads_width : (index + 1) * heads_width] for index in range(4)]
        return (
            layer_output, input_grad, parts[0].T, sums[7, :heads_width], parts[1].T, parts[2].T,
            sums[7, 2 * lanes : 2 * lanes + heads_width], parts[3], sums[5], sums[3], sums[4],
            up_grad, sums[6], down_grad, sums[2], sums[0], sums[1],
        )
    row = shape((width,), F32)
    side_row = shape((heads_width,), F32)
    block = shape((heads_width, width), F32)
    square = shape((width, width), F32)
    results = dict(
        layer_output=shape(frames.shape, BF),
        input_grad=shape(frames.shape, F32),
        query=block,
        query_bias=side_row,
        key=block,
        value=block,
        value_bias=side_row,
        out=block,
        out_bias=row,
        first_gain=row,
        first_shift=row,
        up=square,
        up_bias=row,
        down=square,
        down_bias=row,
        second_gain=row,
        second_shift=row,
    )
    given = ["layer_in", "input_in", "sums", "up_in", "down_in", "heads_in"]
    buffers = dict(
        narrow=pltpu.VMEM((3, count, 2, half, width), BF),
        wide=pltpu.VMEM((3, width, width), F32),
        plain_sem=pltpu.SemaphoreType.DMA((2,)),
        load_sem=pltpu.SemaphoreType.DMA((3,)),
        store_sem=pltpu.SemaphoreType.DMA((8,)),
        layer_stage=pltpu.VMEM(frames.shape, BF),
        input_stage=pltpu.VMEM(frames.shape, F32),
    )
    final = pl.pallas_call(
        functools.partial(widen, 2 * lanes, [*given, *results, *buffers]),
        out_shape=list(results.values()),
        in_specs=[ANY_SPEC] * 2 + [VMEM_SPEC] + [ANY_SPEC] * 3,
        out_specs=[VMEM_SPEC if len(item.shape) == 1 else ANY_SPEC for item in results.values()],
        scratch_shapes=list(buffers.values()),
        compiler_params=pltpu.CompilerParams(vmem_limit_bytes=VMEM_BYTES),
        name="widen",
    )(layer_output, input_grad, sums, *outs[3:])
    final = dict(zip(results, final))
    for name in ("query", "key", "value"):
        final[name] = final[name].T
    return tuple(final.values())


def solution(mesh):
    return jax.shard_map(
        shards,
        mesh=mesh,
        in_specs=(
            P("dp", "tensor", None),
            P("dp", "tensor", None),
            P("dp"),
            P(None, "tensor"),
            P("tensor"),
            P(None, "tensor"),
            P(None, "tensor"),
            P("tensor"),
            P("tensor", None),
            P(),
            P(),
            P(),
            P(None, "tensor"),
            P("tensor"),
            P("tensor", None),
            P(),
            P(),
            P(),
        ),
        out_specs=(
            P("dp", "tensor", None),
            P("dp", "tensor", None),
            P(None, "tensor"),
            P("tensor"),
            P(None, "tensor"),
            P(None, "tensor"),
            P("tensor"),
            P("tensor", None),
            P(),
            P(),
            P(),
            P(None, "tensor"),
            P("tensor"),
            P("tensor", None),
            P(),
            P(),
            P(),
        ),
        check_vma=False,
    )
```

profile of v0, /device:TPU:0, one launch (start us, length us, event | category | flops | bytes accessed | tf_op | source)
XLA Modules:
  0.0 205.4 jit_solution(7801667966830609059)
XLA Ops:
  0.7 198.2 %layer.1 = (bf16[2,200,768]{2,1,0:T(8,128)(2,1)}, f32[2,200,768]{2,1,0:T(8,128)}, f32[8,768]{1,0:T(8,128)}, bf16[8,2,48,768]{3,2,1,0:T(8,128)(2,1)}, bf16[8,2,48...) custom-call(s32[2]{0:T(128)} %refs_0_.1, bf16[2,200,768]{2,1,0:T(8,128)(2,1)} %refs_1_.1, f32[2,200,768]{2,1,0:T(8,128)} %refs_2_.1, ...), custom_call_target="tpu_custom_call" | custom-call | tf_op jit(solution)/shard_map/layer/pallas_call | solution.py:837
  198.9 6.4 %widen.1 = (bf16[2,200,768]{2,1,0:T(8,128)(2,1)}, f32[2,200,768]{2,1,0:T(8,128)}, f32[192,768]{1,0:T(8,128)}, f32[192]{0:T(256)}, f32[192,768]{1,0:T(8,128)}, /*...) custom-call(bf16[2,200,768]{2,1,0:T(8,128)(2,1)} %get-tuple-element., ...), custom_call_target="tpu_custom_call" | custom-call | tf_op jit(solution)/shard_map/widen/pallas_call | solution.py:892
where the time goes:
time: 206 us; the launch traced here: 205 us
  Pallas kernels  205 us (100%)
    pallas_call x1, Pallas kernels, shards(): pl.pallas_call(functools.partial(layer, count if ringed else 0, [*inputs,...  198 us
    pallas_call x1, Pallas kernels, shards(): pl.pallas_call(functools.partial(widen, 2 * lanes, [*given, *results, *bu...  6.37 us

commit v1 on v0

--- a/solution.py
+++ b/solution.py
@@ -15,7 +15,7 @@
 INVERSE_ROOT_TAU = 0.3989422804014327
 MASKED = -1e30
 VMEM_BYTES = 62 << 20
-POLLS = (4, 2, 1, 2, 2, 1)
+POLLS = (3, 2, 1, 2, 2, 1)
 BF = jnp.bfloat16
 F32 = jnp.float32
 
@@ -78,13 +78,14 @@
 
 
 class Gather:
-    def __init__(self, group, full, send, recv):
+    def __init__(self, group, full, send, recv, real):
         self.group, self.full, self.send, self.recv = group, full, send, recv
+        self.real = pl.ds(0, real)
 
     def _copy(self, seq, kind):
         group = self.group
         share = group.far if kind == 2 else group.own
-        slot = self.full.at[seq, share]
+        slot = self.full.at[seq, share, self.real] if kind == 0 else self.full.at[seq, share]
         peer = group.far if kind == 0 else group.mate
         return group.copy(slot, slot, self.send.at[seq, kind], self.recv.at[seq, kind], peer)
 
@@ -112,8 +113,9 @@
 
 
 class Scatter:
-    def __init__(self, group, buffers, send, recv):
+    def __init__(self, group, buffers, send, recv, real):
         self.group = group
+        self.real = pl.ds(0, real)
         self.outgoing, self.keep, self.near, self.cross, self.landed = buffers
         self.send, self.recv = send, recv
 
@@ -128,8 +130,8 @@
 
     def _cross(self, seq):
         return self.group.copy(
-            self.cross.at[seq],
-            self.landed.at[seq],
+            self.cross.at[seq, self.real],
+            self.landed.at[seq, self.real],
             self.send.at[seq, 2],
             self.recv.at[seq, 2],
             self.group.far,
@@ -189,20 +191,20 @@
 
 
 class Ring:
-    def __init__(self, group, count, own, opening, landed, shared, sems, first, rows):
+    def __init__(self, group, count, owns, opening, landed, shared, sends, recvs, first):
         self.group, self.count, self.steps = group, count, count - 1
-        self.own, self.opening, self.landed, self.shared = own, opening, landed, shared
-        self.add_send, self.add_recv, self.share_send, self.share_recv = sems
-        self.half = own.shape[0] // (2 * count)
-        self.first, self.rows = first, rows
-        self.span = pl.ds(first, rows)
+        self.owns, self.opening, self.landed, self.shared = owns, opening, landed, shared
+        self.add_send, self.share_send = sends
+        self.add_recv, self.share_recv = recvs
+        self.half = owns[0].shape[0] // (2 * count)
+        self.first, self.rows = first, landed.shape[3]
         self.place, self.right, self.left = ring_peers(group.dp, count)
 
-    def _own(self, way, step):
+    def _own(self, which, way, step):
         shift = self.count - 1 - step if way == 0 else 1 + step
         chunk = (self.place + shift) % self.count
         start = pl.multiple_of((2 * chunk + way) * self.half + self.first, 16)
-        return self.own[pl.ds(start, self.rows)]
+        return self.owns[which][pl.ds(start, self.rows)]
 
     def _copy(self, source, target, send, recv, way):
         return pltpu.make_async_remote_copy(
@@ -215,38 +217,34 @@
         )
 
     def _add(self, way, step, source=None):
-        target = self.landed.at[way, step, self.span]
+        target = self.landed.at[way, step]
         return self._copy(
-            target if source is None else source,
-            target,
-            self.add_send.at[way, step],
-            self.add_recv.at[way, step],
-            way,
+            target if source is None else source, target, self.add_send, self.add_recv.at[way, step], way
         )
 
     def _share(self, way, step):
         shift = self.count - step if way == 0 else step
-        slot = self.shared.at[(self.place + shift) % self.count, way, self.span]
-        return self._copy(
-            slot, slot, self.share_send.at[way, step], self.share_recv.at[way, step], way
-        )
+        slot = self.shared.at[(self.place + shift) % self.count, way]
+        return self._copy(slot, slot, self.share_send, self.share_recv.at[way, step], way)
 
     def open(self):
         for way in range(2):
-            self.opening[way, self.span] = self._own(way, 0).astype(BF)
-            self._add(way, 0, self.opening.at[way, self.span]).start()
+            for which in range(len(self.owns)):
+                self.opening[way, which] = self._own(which, way, 0).astype(BF)
+            self._add(way, 0, self.opening.at[way]).start()
 
     def advance(self, step):
         last = self.steps - 1
         for way in range(2):
             if step < self.steps:
                 self._add(way, step).wait_recv()
-                total = self.landed[way, step, self.span].astype(F32) + self._own(way, step + 1)
+                target = self.landed.at[way, step] if step < last else self.shared.at[self.place, way]
+                for which in range(len(self.owns)):
+                    total = self.landed[way, step, which].astype(F32) + self._own(which, way, step + 1)
+                    target[which] = total.astype(BF)
                 if step < last:
-                    self.landed[way, step, self.span] = total.astype(BF)
-                    self._add(way, step + 1, self.landed.at[way, step, self.span]).start()
+                    self._add(way, step + 1, target).start()
                 else:
-                    self.shared[self.place, way, self.span] = total.astype(BF)
                     self._share(way, 0).start()
             else:
                 turn = step - self.steps
@@ -254,11 +252,9 @@
                 if turn < last:
                     self._share(way, turn + 1).start()
 
-    def close(self):
-        for way in range(2):
-            for step in range(self.steps):
-                self._add(way, step).wait_send()
-                self._share(way, step).wait_send()
+    def wait_sends(self, landed):
+        for send in (self.add_send, self.share_send):
+            self._copy(landed, landed, send, self.add_recv.at[0, 0], 0).wait_send()
 
 
 def ring_peers(index, count):
@@ -313,6 +309,16 @@
 
 def layer(count, names, *refs):
     r = types.SimpleNamespace(**dict(zip(names, refs)))
+    loads = {
+        name[:-5]: pltpu.make_async_copy(ref, getattr(r, name[:-5]), r.load_sem.at[index])
+        for index, (name, ref) in enumerate(zip(names, refs))
+        if name.endswith("_from")
+    }
+
+    def loaded(*wanted):
+        for name in wanted or list(loads):
+            loads.pop(name).wait()
+
     seqs, share_rows, width = r.frames.shape
     rows = r.full_frames.shape[2]
     length = 4 * rows
@@ -325,21 +331,22 @@
     if count:
         pairs = halving_peers(group.dp, count)
         ring_sides = list(ring_peers(group.dp, count)[1:])
+    tail = pl.ds(share_rows, rows - share_rows)
+    if rows > share_rows:
+        for full in (r.full_frames, r.first_full, r.grad_mixed, r.grad_full):
+            full[:, :, tail] = jnp.zeros_like(full[:, :, tail])
+        r.landed[:, tail] = jnp.zeros_like(r.landed[:, tail])
     met = group.greet(ring_sides + pairs)
 
-    out_bias, first_gain, first_shift, down_bias, second_gain, second_shift, up_bias = (
-        row[...].reshape(1, row.shape[0])
-        for row in (
-            r.out_bias, r.first_gain, r.first_shift, r.down_bias, r.second_gain, r.second_shift, r.up_bias,
-        )
-    )
+    for load in loads.values():
+        load.start()
     buffers = (r.outgoing, r.keep, r.near, r.cross, r.landed)
     gathers = [
-        Gather(group, full, r.gather_send.at[index], r.gather_recv.at[index])
+        Gather(group, full, r.gather_send.at[index], r.gather_recv.at[index], share_rows)
         for index, full in enumerate((r.full_frames, r.first_full, r.grad_mixed, r.grad_full))
     ]
     scatters = [
-        Scatter(group, buffers, r.scatter_send.at[index], r.scatter_recv.at[index])
+        Scatter(group, buffers, r.scatter_send.at[index], r.scatter_recv.at[index], share_rows)
         for index in range(4)
     ]
     grad_total = r.hidden.at[0]
@@ -366,9 +373,11 @@
     def place_frames(seq):
         r.full_frames[seq, group.own] = pad_rows(r.frames[seq].astype(F32), rows).astype(BF)
 
+    loaded("frames")
     each(place_frames)
     met()
     each(gathers[0].start)
+    loaded("query_weight", "key_weight", "value_weight", "query_bias", "value_bias", "out_weight")
     r.wide_weight[...] = jnp.zeros_like(r.wide_weight)
     for index, weight in enumerate((r.query_weight, r.key_weight, r.value_weight)):
         r.wide_weight[index * lanes : index * lanes + heads_width] = weight[...]
@@ -435,6 +444,13 @@
         r.first_full[seq, group.own] = (normed * first_gain + first_shift).astype(BF)
         gathers[1].start(seq)
 
+    loaded()
+    out_bias, first_gain, first_shift, down_bias, second_gain, second_shift, up_bias = (
+        row[...].reshape(1, row.shape[0])
+        for row in (
+            r.out_bias, r.first_gain, r.first_shift, r.down_bias, r.second_gain, r.second_shift, r.up_bias,
+        )
+    )
     each(first_norm)
 
     def feed(seq):
@@ -462,7 +478,7 @@
         r.grad_mixed[seq, group.own] = back.astype(BF)
         gathers[2].start(seq)
         r.grad_rows[seq] = back
-        r.layer_output[seq] = (normed * second_gain + second_shift)[:share_rows].astype(BF)
+        r.output_rows[seq] = (normed * second_gain + second_shift)[:share_rows].astype(BF)
         r.rows_sum[0:1] += sum_rows(grad * normed)
         r.rows_sum[1:2] += sum_rows(grad)
         r.rows_sum[2:3] += sum_rows(back)
@@ -507,10 +523,6 @@
 
     queue = []
 
-    def advance_both(both, step):
-        for ring in both:
-            ring.advance(step)
-
     def poll(times=1):
         for _ in range(times):
             if queue:
@@ -518,36 +530,36 @@
 
     for seq in range(seqs):
         feed_weights(seq)
-        if seq == seqs - 1 and count:
-            half = width // (2 * count)
-
-            def make_ring(index, own, first, size):
-                return Ring(
+    if count:
+        def make_rings(owns, opening, landed, shared, index):
+            return [
+                Ring(
                     group,
                     count,
-                    own,
-                    r.opening.at[index],
-                    r.ring_landed.at[index],
-                    r.ring_shared.at[index],
-                    [
-                        sem.at[index, first // 16]
-                        for sem in (r.add_send, r.add_recv, r.share_send, r.share_recv)
-                    ],
-                    first,
-                    size,
+                    owns,
+                    opening.at[part],
+                    landed.at[part],
+                    shared.at[part],
+                    (r.ring_send.at[index, 0], r.ring_send.at[index, 1]),
+                    (r.ring_recv.at[index, part, 0], r.ring_recv.at[index, part, 1]),
+                    part * landed.shape[4],
                 )
-
-            rings = [
-                make_ring(index, own, first, 16)
-                for first in range(0, half, 16)
-                for index, own in enumerate((r.up_grad, r.down_grad))
+                for part in range(landed.shape[0])
             ]
-            late_rings = [make_ring(2, heads_grad, first, 16) for first in range(0, half, 16)]
+
+        rings = make_rings(
+            (r.up_grad, r.down_grad), r.feed_opening, r.feed_landed, r.feed_shared, 0
+        )
+        late_rings = make_rings(
+            (heads_grad,), r.heads_opening, r.heads_landed, r.heads_shared, 1
+        )
+        for ring in rings:
+            ring.open()
+        for step in range(2 * (count - 1)):
             for ring in rings:
-                ring.open()
-            for step in range(2 * (count - 1)):
-                for first in range(0, len(rings), 2):
-                    queue.append(functools.partial(advance_both, rings[first : first + 2], step))
+                queue.append(functools.partial(ring.advance, step))
+    for seq in range(seqs):
+        poll(POLLS[0])
         first_back(seq)
     poll(POLLS[0])
     if count:
@@ -557,10 +569,18 @@
         totals.begin(0, r.rows_sum[...])
     heads_grad[...] = jnp.zeros_like(heads_grad)
 
+    def output_copy(seq):
+        return pltpu.make_async_copy(r.output_rows.at[seq], r.layer_output.at[seq], r.out_sem.at[3, seq])
+
+    def input_copy(seq):
+        return pltpu.make_async_copy(r.input_rows.at[seq], r.input_grad.at[seq], r.out_sem.at[4, seq])
+
     def store_input(seq):
-        r.input_grad[seq] = (scatters[3].take(seq) + r.grad_rows[seq])[:share_rows]
+        r.input_rows[seq] = (scatters[3].take(seq) + r.grad_rows[seq])[:share_rows]
+        input_copy(seq).start()
 
     for seq in range(seqs):
+        output_copy(seq).start()
 
         def step(turn):
             gathers[3].wait(seq, turn)
@@ -628,8 +648,10 @@
         place = lax.broadcasted_iota(jnp.int32, r.rows_sum.shape, 0)
         totals.begin(2, jnp.where(place == 7, r.rows_sum[...], totals.end(1)))
         copies = [
-            pltpu.make_async_copy(r.ring_shared.at[index], out, r.out_sem.at[index])
-            for index, out in enumerate((r.up_sum, r.down_sum, r.heads_sum))
+            pltpu.make_async_copy(shared, out, r.out_sem.at[index, 0])
+            for index, (shared, out) in enumerate(
+                ((r.feed_shared, r.feed_sum), (r.heads_shared, r.heads_sum))
+            )
         ]
         level = 2
         last = len(pairs) + 1
@@ -649,13 +671,13 @@
         poll(len(queue))
         for copy in copies:
             copy.start()
-        for ring in rings + late_rings:
-            ring.close()
+        rings[0].wait_sends(r.feed_landed)
+        late_rings[0].wait_sends(r.heads_landed)
     else:
         store_input(seqs - 1)
         r.sums[...] = r.rows_sum[...]
         copies = [
-            pltpu.make_async_copy(own, out, r.out_sem.at[index])
+            pltpu.make_async_copy(own, out, r.out_sem.at[index, 0])
             for index, (own, out) in enumerate(
                 ((r.up_grad, r.up_sum), (r.down_grad, r.down_sum), (heads_grad, r.heads_sum))
             )
@@ -665,6 +687,8 @@
     for seq in range(seqs):
         for gather in gathers:
             gather.close(seq)
+        output_copy(seq).wait()
+        input_copy(seq).wait()
     for copy in copies:
         copy.wait()
 
@@ -685,15 +709,24 @@
         pltpu.make_async_copy(source, stage, r.plain_sem.at[index])
         for index, (source, stage, _) in enumerate(plain)
     ]
-    loads = [
-        pltpu.make_async_copy(source, r.narrow.at[index], r.load_sem.at[index])
-        for index, source in enumerate((r.up_in, r.down_in, r.heads_in))
-    ]
-    for copy in loads + plain_loads:
+    loads = []
+    for index, (source, which) in enumerate(((r.feed_in, 0), (r.feed_in, 1), (r.heads_in, 0))):
+        loads.append(
+            [
+                pltpu.make_async_copy(
+                    source.at[part, :, :, which],
+                    r.narrow.at[index, :, :, pl.ds(part * 16, 16)],
+                    r.load_sem.at[index, part],
+                )
+                for part in range(source.shape[0])
+            ]
+        )
+    for copy in sum(loads, plain_loads):
         copy.start()
     stores = []
-    for index, load in enumerate(loads):
-        load.wait()
+    for index, pieces in enumerate(loads):
+        for load in pieces:
+            load.wait()
         r.wide[index] = r.narrow[index].astype(F32).reshape(width, width)
         if index < 2:
             parts = [(r.wide.at[index], (r.up, r.down)[index])]
@@ -776,17 +809,20 @@
         second_gain=second_gain,
         second_shift=second_shift,
     )
-    summed = (
-        shape((count, 2, half, width), BF) if ringed else shape((width, width), F32)
-    )
     outputs = dict(
         layer_output=shape(frames.shape, BF),
         input_grad=shape(frames.shape, F32),
         sums=shape((8, width), F32),
-        up_sum=summed,
-        down_sum=summed,
-        heads_sum=summed,
-    )
+    )
+    if ringed:
+        outputs.update(
+            feed_sum=shape((half // 16, count, 2, 2, 16, width), BF),
+            heads_sum=shape((half // 16, count, 2, 1, 16, width), BF),
+        )
+    else:
+        outputs.update(
+            {name: shape((width, width), F32) for name in ("up_sum", "down_sum", "heads_sum")}
+        )
     scratch = dict(
         wide_weight=pltpu.VMEM((3 * lanes, width), BF),
         wide_out=pltpu.VMEM((lanes, width), BF),
@@ -817,28 +853,36 @@
         gather_recv=pltpu.SemaphoreType.DMA((4, seqs, 3)),
         scatter_send=pltpu.SemaphoreType.DMA((4, seqs, 3)),
         scatter_recv=pltpu.SemaphoreType.DMA((4, seqs, 3)),
-        out_sem=pltpu.SemaphoreType.DMA((3,)),
-    )
+        out_sem=pltpu.SemaphoreType.DMA((5, seqs)),
+        load_sem=pltpu.SemaphoreType.DMA((len(inputs),)),
+        output_rows=pltpu.VMEM(frames.shape, BF),
+        input_rows=pltpu.VMEM(frames.shape, F32),
+    )
+    scratch.update(
+        {name: pltpu.VMEM(item.shape, item.dtype) for name, item in inputs.items() if name != "lengths"}
+    )
+    given = [name if name == "lengths" else name + "_from" for name in inputs]
     if ringed:
-        ring_sem = pltpu.SemaphoreType.DMA((3, half // 16, 2, count - 1))
+        parts = half // 16
         scratch.update(
-            opening=pltpu.VMEM((3, 2, half, width), BF),
-            ring_landed=pltpu.VMEM((3, 2, count - 1, half, width), BF),
-            ring_shared=pltpu.VMEM((3, count, 2, half, width), BF),
-            add_send=ring_sem,
-            add_recv=ring_sem,
-            share_send=ring_sem,
-            share_recv=ring_sem,
+            feed_opening=pltpu.VMEM((parts, 2, 2, 16, width), BF),
+            heads_opening=pltpu.VMEM((parts, 2, 1, 16, width), BF),
+            feed_landed=pltpu.VMEM((parts, 2, count - 1, 2, 16, width), BF),
+            heads_landed=pltpu.VMEM((parts, 2, count - 1, 1, 16, width), BF),
+            feed_shared=pltpu.VMEM((parts, count, 2, 2, 16, width), BF),
+            heads_shared=pltpu.VMEM((parts, count, 2, 1, 16, width), BF),
+            ring_send=pltpu.SemaphoreType.DMA((2, 2)),
+            ring_recv=pltpu.SemaphoreType.DMA((2, parts, 2, 2, count - 1)),
             small_out=pltpu.VMEM((levels, 8, width), F32),
             small_in=pltpu.VMEM((levels, 8, width), F32),
             small_send=pltpu.SemaphoreType.DMA((levels,)),
             small_recv=pltpu.SemaphoreType.DMA((levels,)),
         )
     outs = pl.pallas_call(
-        functools.partial(layer, count if ringed else 0, [*inputs, *outputs, *scratch]),
+        functools.partial(layer, count if ringed else 0, [*given, *outputs, *scratch]),
         out_shape=list(outputs.values()),
-        in_specs=[pl.BlockSpec(memory_space=pltpu.SMEM)] + [VMEM_SPEC] * (len(inputs) - 1),
-        out_specs=[VMEM_SPEC] * 3 + [ANY_SPEC] * 3,
+        in_specs=[pl.BlockSpec(memory_space=pltpu.SMEM)] + [ANY_SPEC] * (len(inputs) - 1),
+        out_specs=[VMEM_SPEC if name == "sums" else ANY_SPEC for name in outputs],
         scratch_shapes=list(scratch.values()),
         compiler_params=pltpu.CompilerParams(
             collective_id=0, has_side_effects=True, vmem_limit_bytes=VMEM_BYTES
@@ -879,12 +923,12 @@
         second_gain=row,
         second_shift=row,
     )
-    given = ["layer_in", "input_in", "sums", "up_in", "down_in", "heads_in"]
+    given = ["layer_in", "input_in", "sums", "feed_in", "heads_in"]
     buffers = dict(
         narrow=pltpu.VMEM((3, count, 2, half, width), BF),
         wide=pltpu.VMEM((3, width, width), F32),
         plain_sem=pltpu.SemaphoreType.DMA((2,)),
-        load_sem=pltpu.SemaphoreType.DMA((3,)),
+        load_sem=pltpu.SemaphoreType.DMA((3, half // 16)),
         store_sem=pltpu.SemaphoreType.DMA((8,)),
         layer_stage=pltpu.VMEM(frames.shape, BF),
         input_stage=pltpu.VMEM(frames.shape, F32),
@@ -892,7 +936,7 @@
     final = pl.pallas_call(
         functools.partial(widen, 2 * lanes, [*given, *results, *buffers]),
         out_shape=list(results.values()),
-        in_specs=[ANY_SPEC] * 2 + [VMEM_SPEC] + [ANY_SPEC] * 3,
+        in_specs=[ANY_SPEC] * 2 + [VMEM_SPEC] + [ANY_SPEC] * 2,
         out_specs=[VMEM_SPEC if len(item.shape) == 1 else ANY_SPEC for item in results.values()],
         scratch_shapes=list(buffers.values()),
         compiler_params=pltpu.CompilerParams(vmem_limit_bytes=VMEM_BYTES),

time: 206 us -> 199 us (0.966)
  Pallas kernels: 205 us -> 198 us
    pallas_call x1, Pallas kernels: 198 us -> 192 us  [shards(): pl.pallas_call(functools.partial(layer, count if ringed else 0, [*given,...]
where the time goes in v1:
time: 199 us
  Pallas kernels  198 us (99%)
    pallas_call x1, Pallas kernels, shards(): pl.pallas_call(functools.partial(layer, count if ringed else 0, [*given,...  192 us
    pallas_call x1, Pallas kernels, shards(): pl.pallas_call(functools.partial(widen, 2 * lanes, [*given, *results, *bu...  6.39 us

profile of v1, /device:TPU:0, one launch (start us, length us, event | category | flops | bytes accessed | tf_op | source)
XLA Modules:
  0.0 199.1 jit_solution(990970597455216644)
XLA Ops:
  0.7 191.8 %layer.1 = (bf16[2,200,768]{2,1,0:T(8,128)(2,1)}, f32[2,200,768]{2,1,0:T(8,128)}, f32[8,768]{1,0:T(8,128)}, bf16[3,8,2,2,16,768]{5,4,3,2,1,0:T(8,128)(2,1)}, bf16[3,8,2,1,16,768]{5,4,3,2,1,0:T(8,128)(2,1)}) custom-call(s32[2]{0:T(128)} %refs_0_.1, bf16[2,200,768]{2,1,0:T(8,128)(2,1)} %refs_1_.1, f32[2,200,768]{2,1,0:T(8,128)} %refs_2_.1, ...), custom_call_target="tpu_custom_call" | custom-call | tf_op jit(solution)/shard_map/layer/pallas_call | solution.py:881
  192.5 6.4 %widen.1 = (bf16[2,200,768]{2,1,0:T(8,128)(2,1)}, f32[2,200,768]{2,1,0:T(8,128)}, f32[192,768]{1,0:T(8,128)}, f32[192]{0:T(256)}, f32[192,768]{1,0:T(8,128)}, /*...) custom-call(bf16[2,200,768]{2,1,0:T(8,128)(2,1)} %get-tuple-element., ...), custom_call_target="tpu_custom_call" | custom-call | tf_op jit(solution)/shard_map/widen/pallas_call | solution.py:936

commit v2 on v1

--- a/solution.py
+++ b/solution.py
@@ -15,7 +15,10 @@
 INVERSE_ROOT_TAU = 0.3989422804014327
 MASKED = -1e30
 VMEM_BYTES = 62 << 20
-POLLS = (3, 2, 1, 2, 2, 1)
+POLLS = (3, 1, 0, 1, 1, 1, 2)
+TAIL = (
+    (1, 1), (0, 3), (2, 1), (1, 2), (3, 1), (2, 2), (1, 3), (3, 2), (2, 3), (3, 3),
+)
 BF = jnp.bfloat16
 F32 = jnp.float32
 
@@ -257,6 +260,82 @@
             self._copy(landed, landed, send, self.add_recv.at[0, 0], 0).wait_send()
 
 
+class Pairwise:
+    def __init__(self, group, count, terms, outgoing, half, quarter, shared, send, recv):
+        self.group, self.spots = group, count // 2
+        self.terms, self.outgoing, self.half, self.quarter = terms, outgoing, half, quarter
+        self.shared, self.send, self.recv = shared, send, recv
+        self.arrays = half.shape[1]
+        self.spot, self.side = group.dp // 2, group.dp % 2
+
+    def _copy(self, source, target, index, spot, side):
+        return pltpu.make_async_remote_copy(
+            src_ref=source,
+            dst_ref=target,
+            send_sem=self.send.at[index],
+            recv_sem=self.recv.at[index],
+            device_id=(spot * 2 + side, self.group.own),
+            device_id_type=MESH,
+        )
+
+    def _out(self):
+        return self._copy(self.outgoing, self.half, 0, self.spot, 1 - self.side)
+
+    def _add(self, offset):
+        spot = (self.spot + offset) % self.spots
+        return self._copy(
+            self.half.at[spot], self.quarter.at[offset - 1], offset, spot, self.side
+        )
+
+    def _share(self, offset):
+        spot = (self.spot + offset) % self.spots
+        slot = self.shared.at[self.side, self.spot]
+        return self._copy(slot, slot, self.spots - 1 + offset, spot, self.side)
+
+    def _back(self):
+        slot = self.shared.at[self.side]
+        return self._copy(slot, slot, 2 * self.spots - 1, self.spot, 1 - self.side)
+
+    def act(self, phase):
+        others = range(1, self.spots)
+        if phase == 0:
+            for spot in range(self.spots):
+                for which in range(self.arrays):
+                    self.outgoing[spot, which] = self.terms(which, 1 - self.side, spot).astype(BF)
+            self._out().start()
+        elif phase == 1:
+            self._out().wait_recv()
+            for offset in others:
+                spot = (self.spot + offset) % self.spots
+                for which in range(self.arrays):
+                    total = self.half[spot, which].astype(F32) + self.terms(which, self.side, spot)
+                    self.half[spot, which] = total.astype(BF)
+                self._add(offset).start()
+        elif phase == 2:
+            for offset in others:
+                self._add(offset).wait_recv()
+            for which in range(self.arrays):
+                total = self.half[self.spot, which].astype(F32) + self.terms(
+                    which, self.side, self.spot
+                )
+                for offset in others:
+                    total = total + self.quarter[offset - 1, which].astype(F32)
+                self.shared[self.side, self.spot, which] = total.astype(BF)
+            for offset in others:
+                self._share(offset).start()
+        elif phase == 3:
+            for offset in others:
+                self._share(offset).wait_recv()
+            self._back().start()
+        else:
+            self._back().wait_recv()
+            self._out().wait_send()
+            self._back().wait_send()
+            for offset in others:
+                self._add(offset).wait_send()
+                self._share(offset).wait_send()
+
+
 def ring_peers(index, count):
     odd = index % 2
     place = (1 - odd) * (index // 2) + odd * (count - 1 - index // 2)
@@ -331,6 +410,9 @@
     if count:
         pairs = halving_peers(group.dp, count)
         ring_sides = list(ring_peers(group.dp, count)[1:])
+        ring_sides += [
+            (group.dp + 2 * offset) % count for offset in range(1, count // 2)
+        ]
     tail = pl.ds(share_rows, rows - share_rows)
     if rows > share_rows:
         for full in (r.full_frames, r.first_full, r.grad_mixed, r.grad_full):
@@ -351,7 +433,6 @@
     ]
     grad_total = r.hidden.at[0]
     heads_grad = r.hidden.at[1, pl.ds(0, 4 * heads_width)]
-    grad_projected = r.activated.at[0]
 
     def each(stage):
         def body(seq, carry):
@@ -478,7 +559,7 @@
         r.grad_mixed[seq, group.own] = back.astype(BF)
         gathers[2].start(seq)
         r.grad_rows[seq] = back
-        r.output_rows[seq] = (normed * second_gain + second_shift)[:share_rows].astype(BF)
+        r.frames[seq] = (normed * second_gain + second_shift)[:share_rows].astype(BF)
         r.rows_sum[0:1] += sum_rows(grad * normed)
         r.rows_sum[1:2] += sum_rows(grad)
         r.rows_sum[2:3] += sum_rows(back)
@@ -527,6 +608,10 @@
         for _ in range(times):
             if queue:
                 queue.pop(0)()
+
+    def act(part, phase):
+        if count:
+            pieces[part].act(phase)
 
     for seq in range(seqs):
         feed_weights(seq)
@@ -550,9 +635,24 @@
         rings = make_rings(
             (r.up_grad, r.down_grad), r.feed_opening, r.feed_landed, r.feed_shared, 0
         )
-        late_rings = make_rings(
-            (heads_grad,), r.heads_opening, r.heads_landed, r.heads_shared, 1
-        )
+        def heads_terms(first, size, which, side, spot):
+            start = first + (side * (count // 2) + spot) * size
+            return heads_grad[pl.ds(pl.multiple_of(start, 8), size)]
+
+        pieces = [
+            Pairwise(
+                group,
+                count,
+                functools.partial(heads_terms, part * heads_width, r.heads_half.shape[3]),
+                r.heads_out.at[part],
+                r.heads_half.at[part],
+                r.heads_quarter.at[part],
+                r.heads_shared.at[part],
+                r.pair_send.at[part],
+                r.pair_recv.at[part],
+            )
+            for part in range(1 + heads)
+        ]
         for ring in rings:
             ring.open()
         for step in range(2 * (count - 1)):
@@ -567,16 +667,14 @@
             group, pairs, r.small_out, r.small_in, r.small_send, r.small_recv, 6
         )
         totals.begin(0, r.rows_sum[...])
-    heads_grad[...] = jnp.zeros_like(heads_grad)
-
     def output_copy(seq):
-        return pltpu.make_async_copy(r.output_rows.at[seq], r.layer_output.at[seq], r.out_sem.at[3, seq])
+        return pltpu.make_async_copy(r.frames.at[seq], r.layer_output.at[seq], r.out_sem.at[3, seq])
 
     def input_copy(seq):
-        return pltpu.make_async_copy(r.input_rows.at[seq], r.input_grad.at[seq], r.out_sem.at[4, seq])
+        return pltpu.make_async_copy(r.cotangent.at[seq], r.input_grad.at[seq], r.out_sem.at[4, seq])
 
     def store_input(seq):
-        r.input_rows[seq] = (scatters[3].take(seq) + r.grad_rows[seq])[:share_rows]
+        r.cotangent[seq] = (scatters[3].take(seq) + r.grad_rows[seq])[:share_rows]
         input_copy(seq).start()
 
     for seq in range(seqs):
@@ -586,11 +684,15 @@
             gathers[3].wait(seq, turn)
             share = group.share(turn)
             r.grad_context[at_share(share)] = dot_nt(r.grad_full[seq, share], r.wide_out[...]).astype(BF)
-            heads_grad[3 * heads_width :] += dot_tn(
-                r.context[seq, at_share(share)], r.grad_full[seq, share]
-            )[:heads_width]
 
         turns(step)
+        part = dot_tn(r.context[seq], r.grad_full[seq].reshape(length, width))[:heads_width]
+        if seq == 0:
+            heads_grad[:heads_width] = part
+        else:
+            heads_grad[:heads_width] += part
+        if seq == seqs - 1:
+            act(0, 0)
         poll(POLLS[1])
         grad_total[...] = jnp.zeros_like(grad_total)
         keys = r.projected[seq, :, lanes : 2 * lanes]
@@ -619,22 +721,33 @@
             grad_total[:, span] = jnp.where(inside, part, grad_total[:, span])
             span = slice(head * HEAD_DIM, (head + 1) * HEAD_DIM)
             grad_total[:, span] = jnp.transpose(dot(key_columns[span], slopes))
+            block = slice((1 + head) * heads_width, (2 + head) * heads_width)
+            columns = jnp.concatenate(
+                [
+                    grad_total[:, index * lanes + head * HEAD_DIM : index * lanes + (head + 1) * HEAD_DIM]
+                    for index in range(3)
+                ],
+                axis=1,
+            ).astype(BF)
+            part = dot_tn(columns, r.full_frames[seq].reshape(length, width))
+            if seq == 0:
+                heads_grad[block] = part
+            else:
+                heads_grad[block] += part
+            if seq == seqs - 1:
+                act(1 + head, 0)
+                if head:
+                    act(0, head)
             poll(POLLS[3])
 
         def finish(turn):
             share = group.share(turn)
             grads = grad_total[at_share(share)].astype(BF)
-            grad_projected[at_share(share)] = grads
             r.rows_sum[7:8] += sum_rows(grads.astype(F32))
             scatters[3].put(seq, turn, dot(grads, r.wide_weight[...]))
 
         turns(finish)
         poll(POLLS[4])
-        for index in range(3):
-            heads_grad[index * heads_width : (index + 1) * heads_width] += dot_tn(
-                grad_projected[:, index * lanes : (index + 1) * lanes],
-                r.full_frames[seq].reshape(length, width),
-            )[:heads_width]
         poll(POLLS[5])
         if seq == 0:
             if count:
@@ -643,8 +756,6 @@
             store_input(seq - 1)
 
     if count:
-        for ring in late_rings:
-            ring.open()
         place = lax.broadcasted_iota(jnp.int32, r.rows_sum.shape, 0)
         totals.begin(2, jnp.where(place == 7, r.rows_sum[...], totals.end(1)))
         copies = [
@@ -655,13 +766,12 @@
         ]
         level = 2
         last = len(pairs) + 1
-        for step in range(2 * (count - 1)):
-            for ring in late_rings:
-                ring.advance(step)
-                poll()
-            if step == 2:
+        for at, (part, phase) in enumerate(TAIL):
+            pieces[part].act(phase)
+            poll(POLLS[6])
+            if at == 1:
                 store_input(seqs - 1)
-            if step % 3 == 2 and level <= last:
+            if at % 2 == 1 and level <= last:
                 rows_total = totals.end(level)
                 level += 1
                 if level <= last:
@@ -669,10 +779,11 @@
                 else:
                     r.sums[...] = rows_total
         poll(len(queue))
+        for piece in pieces:
+            piece.act(4)
         for copy in copies:
             copy.start()
         rings[0].wait_sends(r.feed_landed)
-        late_rings[0].wait_sends(r.heads_landed)
     else:
         store_input(seqs - 1)
         r.sums[...] = r.rows_sum[...]
@@ -710,7 +821,7 @@
         for index, (source, stage, _) in enumerate(plain)
     ]
     loads = []
-    for index, (source, which) in enumerate(((r.feed_in, 0), (r.feed_in, 1), (r.heads_in, 0))):
+    for index, (source, which) in enumerate(((r.feed_in, 0), (r.feed_in, 1))):
         loads.append(
             [
                 pltpu.make_async_copy(
@@ -721,24 +832,34 @@
                 for part in range(source.shape[0])
             ]
         )
-    for copy in sum(loads, plain_loads):
+    heads_load = pltpu.make_async_copy(r.heads_in, r.heads, r.plain_sem.at[2])
+    for copy in sum(loads, plain_loads + [heads_load]):
         copy.start()
     stores = []
     for index, pieces in enumerate(loads):
         for load in pieces:
             load.wait()
         r.wide[index] = r.narrow[index].astype(F32).reshape(width, width)
-        if index < 2:
-            parts = [(r.wide.at[index], (r.up, r.down)[index])]
-        else:
-            parts = [
-                (r.wide.at[index, pl.ds(part * heads_width, heads_width)], target)
-                for part, target in enumerate((r.query, r.key, r.value, r.out))
+        store = pltpu.make_async_copy(r.wide.at[index], (r.up, r.down)[index], r.store_sem.at[len(stores)])
+        store.start()
+        stores.append(store)
+    heads_load.wait()
+    heads = heads_width // HEAD_DIM
+    for piece in range(1 + heads):
+        rows = r.heads[piece].astype(F32).reshape(heads_width, width)
+        for kind in range(3):
+            place = 3 * heads + kind if piece == 0 else kind * heads + piece - 1
+            r.wide[2, place * HEAD_DIM : (place + 1) * HEAD_DIM] = rows[
+                kind * HEAD_DIM : (kind + 1) * HEAD_DIM
             ]
-        for source, target in parts:
-            store = pltpu.make_async_copy(source, target, r.store_sem.at[len(stores)])
-            store.start()
-            stores.append(store)
+    parts = [
+        (r.wide.at[2, pl.ds(part * heads_width, heads_width)], target)
+        for part, target in enumerate((r.query, r.key, r.value, r.out))
+    ]
+    for source, target in parts:
+        store = pltpu.make_async_copy(source, target, r.store_sem.at[len(stores)])
+        store.start()
+        stores.append(store)
     for load, (_, stage, target) in zip(plain_loads, plain):
         load.wait()
         store = pltpu.make_async_copy(stage, target, r.store_sem.at[len(stores)])
@@ -783,8 +904,10 @@
     lanes = up_to(heads_width + 1, 128)
     shape = jax.ShapeDtypeStruct
     count = lax.axis_size("dp")
-    ringed = count & (count - 1) == 0 and width % (32 * count) == 0
+    ringed = count & (count - 1) == 0 and width % (32 * count) == 0 and count >= 4
+    ringed = ringed and heads_width == 3 * HEAD_DIM and heads_width % (8 * count) == 0
     half = width // (2 * count)
+    heads_parts = 1 + heads_width // HEAD_DIM
     levels = 2 + count.bit_length() - 1
     full = pltpu.VMEM((seqs, 4, rows, width), BF)
     part = pltpu.VMEM((seqs, rows, width), BF)
@@ -817,7 +940,7 @@
     if ringed:
         outputs.update(
             feed_sum=shape((half // 16, count, 2, 2, 16, width), BF),
-            heads_sum=shape((half // 16, count, 2, 1, 16, width), BF),
+            heads_sum=shape((heads_parts, 2, count // 2, 1, heads_width // count, width), BF),
         )
     else:
         outputs.update(
@@ -855,8 +978,6 @@
         scatter_recv=pltpu.SemaphoreType.DMA((4, seqs, 3)),
         out_sem=pltpu.SemaphoreType.DMA((5, seqs)),
         load_sem=pltpu.SemaphoreType.DMA((len(inputs),)),
-        output_rows=pltpu.VMEM(frames.shape, BF),
-        input_rows=pltpu.VMEM(frames.shape, F32),
     )
     scratch.update(
         {name: pltpu.VMEM(item.shape, item.dtype) for name, item in inputs.items() if name != "lengths"}
@@ -864,15 +985,19 @@
     given = [name if name == "lengths" else name + "_from" for name in inputs]
     if ringed:
         parts = half // 16
+        spots, small = count // 2, heads_width // count
         scratch.update(
             feed_opening=pltpu.VMEM((parts, 2, 2, 16, width), BF),
-            heads_opening=pltpu.VMEM((parts, 2, 1, 16, width), BF),
+            heads_out=pltpu.VMEM((heads_parts, spots, 1, small, width), BF),
+            heads_half=pltpu.VMEM((heads_parts, spots, 1, small, width), BF),
             feed_landed=pltpu.VMEM((parts, 2, count - 1, 2, 16, width), BF),
-            heads_landed=pltpu.VMEM((parts, 2, count - 1, 1, 16, width), BF),
+            heads_quarter=pltpu.VMEM((heads_parts, spots - 1, 1, small, width), BF),
             feed_shared=pltpu.VMEM((parts, count, 2, 2, 16, width), BF),
-            heads_shared=pltpu.VMEM((parts, count, 2, 1, 16, width), BF),
-            ring_send=pltpu.SemaphoreType.DMA((2, 2)),
-            ring_recv=pltpu.SemaphoreType.DMA((2, parts, 2, 2, count - 1)),
+            heads_shared=pltpu.VMEM((heads_parts, 2, spots, 1, small, width), BF),
+            pair_send=pltpu.SemaphoreType.DMA((heads_parts, 2 * spots)),
+            pair_recv=pltpu.SemaphoreType.DMA((heads_parts, 2 * spots)),
+            ring_send=pltpu.SemaphoreType.DMA((1, 2)),
+            ring_recv=pltpu.SemaphoreType.DMA((1, parts, 2, 2, count - 1)),
             small_out=pltpu.VMEM((levels, 8, width), F32),
             small_in=pltpu.VMEM((levels, 8, width), F32),
             small_send=pltpu.SemaphoreType.DMA((levels,)),
@@ -894,7 +1019,9 @@
         up_grad, down_grad, heads_grad = lax.psum(tuple(outs[3:]), "dp")
         sums = lax.psum(sums, "dp")
         sums = jnp.concatenate([lax.psum(sums[:6], "tensor"), sums[6:]])
-        parts = [heads_grad[index * heads_width : (index + 1) * heads_width] for index in range(4)]
+        mixed = heads_grad[heads_width:].reshape(-1, 3, HEAD_DIM, width)
+        parts = [mixed[:, index].reshape(heads_width, width) for index in range(3)]
+        parts.append(heads_grad[:heads_width])
         return (
             layer_output, input_grad, parts[0].T, sums[7, :heads_width], parts[1].T, parts[2].T,
             sums[7, 2 * lanes : 2 * lanes + heads_width], parts[3], sums[5], sums[3], sums[4],
@@ -925,10 +1052,11 @@
     )
     given = ["layer_in", "input_in", "sums", "feed_in", "heads_in"]
     buffers = dict(
-        narrow=pltpu.VMEM((3, count, 2, half, width), BF),
+        narrow=pltpu.VMEM((2, count, 2, half, width), BF),
+        heads=pltpu.VMEM(outs[4].shape, BF),
         wide=pltpu.VMEM((3, width, width), F32),
-        plain_sem=pltpu.SemaphoreType.DMA((2,)),
-        load_sem=pltpu.SemaphoreType.DMA((3, half // 16)),
+        plain_sem=pltpu.SemaphoreType.DMA((3,)),
+        load_sem=pltpu.SemaphoreType.DMA((2, half // 16)),
         store_sem=pltpu.SemaphoreType.DMA((8,)),
         layer_stage=pltpu.VMEM(frames.shape, BF),
         input_stage=pltpu.VMEM(frames.shape, F32),

time: 199 us -> 196 us (0.985)
  Pallas kernels: 198 us -> 195 us
    pallas_call x1, Pallas kernels: 192 us -> 188 us  [shards(): pl.pallas_call(functools.partial(layer, count if ringed else 0, [*given,...]
where the time goes in v2:
time: 196 us
  Pallas kernels  195 us (99%)
    pallas_call x1, Pallas kernels, shards(): pl.pallas_call(functools.partial(layer, count if ringed else 0, [*given,...  188 us
    pallas_call x1, Pallas kernels, shards(): pl.pallas_call(functools.partial(widen, 2 * lanes, [*given, *results, *bu...  7.44 us

profile of v2, /device:TPU:0, one launch (start us, length us, event | category | flops | bytes accessed | tf_op | source)
XLA Modules:
  0.0 195.9 jit_solution(14704978405888120968)
XLA Ops:
  0.7 187.6 %layer.1 = (bf16[2,200,768]{2,1,0:T(8,128)(2,1)}, f32[2,200,768]{2,1,0:T(8,128)}, f32[8,768]{1,0:T(8,128)}, bf16[3,8,2,2,16,768]{5,4,3,2,1,0:T(8,128)(2,1)}, bf16[4,2,4,1,24,768]{5,4,3,2,1,0:T(8,128)(2,1)}) custom-call(s32[2]{0:T(128)} %refs_0_.1, bf16[2,200,768]{2,1,0:T(8,128)(2,1)} %refs_1_.1, f32[2,200,768]{2,1,0:T(8,128)} %refs_2_.1, ...), custom_call_target="tpu_custom_call" | custom-call | tf_op jit(solution)/shard_map/layer/pallas_call | solution.py:1006
  188.3 7.4 %widen.1 = (bf16[2,200,768]{2,1,0:T(8,128)(2,1)}, f32[2,200,768]{2,1,0:T(8,128)}, f32[192,768]{1,0:T(8,128)}, f32[192]{0:T(256)}, f32[192,768]{1,0:T(8,128)}, /*...) custom-call(bf16[2,200,768]{2,1,0:T(8,128)(2,1)} %get-tuple-element., ...), custom_call_target="tpu_custom_call" | custom-call | tf_op jit(solution)/shard_map/widen/pallas_call | solution.py:1064

commit v3 on v2

--- a/solution.py
+++ b/solution.py
@@ -15,7 +15,7 @@
 INVERSE_ROOT_TAU = 0.3989422804014327
 MASKED = -1e30
 VMEM_BYTES = 62 << 20
-POLLS = (3, 1, 0, 1, 1, 1, 2)
+POLLS = (1, 1, 0, 1, 1, 1, 1, 1)
 TAIL = (
     (1, 1), (0, 3), (2, 1), (1, 2), (3, 1), (2, 2), (1, 3), (3, 2), (2, 3), (3, 3),
 )
@@ -566,9 +566,10 @@
 
     each(second_norm)
 
-    def feed_back(seq):
+    def feed_back(seq, waited):
         def step(turn):
-            gathers[2].wait(seq, turn)
+            if not waited:
+                gathers[2].wait(seq, turn)
             share = group.share(turn)
             grad_active = dot_nt(r.grad_mixed[seq, share], r.down_weight[...])
             inner = r.hidden[seq, at_share(share)]
@@ -583,11 +584,12 @@
 
         turns(step)
 
-    each(feed_back)
-
-    def feed_weights(seq):
+
+    def down_weights(seq):
         down = dot_tn(r.activated[seq], r.grad_mixed[seq].reshape(length, width))
         r.down_grad[...] = down if seq == 0 else r.down_grad[...] + down
+
+    def up_weights(seq):
         up = dot_tn(r.first_full[seq].reshape(length, width), r.grad_hidden[seq])
         r.up_grad[...] = up if seq == 0 else r.up_grad[...] + up
 
@@ -613,28 +615,22 @@
         if count:
             pieces[part].act(phase)
 
-    for seq in range(seqs):
-        feed_weights(seq)
     if count:
-        def make_rings(owns, opening, landed, shared, index):
-            return [
-                Ring(
-                    group,
-                    count,
-                    owns,
-                    opening.at[part],
-                    landed.at[part],
-                    shared.at[part],
-                    (r.ring_send.at[index, 0], r.ring_send.at[index, 1]),
-                    (r.ring_recv.at[index, part, 0], r.ring_recv.at[index, part, 1]),
-                    part * landed.shape[4],
-                )
-                for part in range(landed.shape[0])
-            ]
-
-        rings = make_rings(
-            (r.up_grad, r.down_grad), r.feed_opening, r.feed_landed, r.feed_shared, 0
-        )
+        rings = [
+            Ring(
+                group,
+                count,
+                (own,),
+                r.feed_opening.at[part],
+                r.feed_landed.at[part],
+                r.feed_shared.at[part],
+                (r.ring_send.at[0], r.ring_send.at[1]),
+                (r.ring_recv.at[part, 0], r.ring_recv.at[part, 1]),
+                0,
+            )
+            for part, own in enumerate((r.up_grad, r.down_grad))
+        ]
+
         def heads_terms(first, size, which, side, spot):
             start = first + (side * (count // 2) + spot) * size
             return heads_grad[pl.ds(pl.multiple_of(start, 8), size)]
@@ -653,11 +649,30 @@
             )
             for part in range(1 + heads)
         ]
-        for ring in rings:
-            ring.open()
-        for step in range(2 * (count - 1)):
-            for ring in rings:
-                queue.append(functools.partial(ring.advance, step))
+
+    def join(part):
+        if count:
+            rings[part].open()
+            waiting = list(queue)
+            queue.clear()
+            for step in range(2 * (count - 1)):
+                queue.extend(waiting[step : step + 1])
+                queue.append(functools.partial(rings[part].advance, step))
+
+    for seq in range(seqs):
+        if seq == seqs - 1:
+            for turn in range(3):
+                gathers[2].wait(seq, turn)
+            down_weights(seq)
+            join(1)
+            feed_back(seq, True)
+        else:
+            feed_back(seq, False)
+            down_weights(seq)
+    poll(POLLS[7])
+    for seq in range(seqs):
+        up_weights(seq)
+    join(0)
     for seq in range(seqs):
         poll(POLLS[0])
         first_back(seq)
@@ -820,25 +835,21 @@
         pltpu.make_async_copy(source, stage, r.plain_sem.at[index])
         for index, (source, stage, _) in enumerate(plain)
     ]
-    loads = []
-    for index, (source, which) in enumerate(((r.feed_in, 0), (r.feed_in, 1))):
-        loads.append(
-            [
-                pltpu.make_async_copy(
-                    source.at[part, :, :, which],
-                    r.narrow.at[index, :, :, pl.ds(part * 16, 16)],
-                    r.load_sem.at[index, part],
-                )
-                for part in range(source.shape[0])
-            ]
-        )
+    loads = [
+        pltpu.make_async_copy(r.feed_in.at[index, :, :, 0], r.narrow.at[index], r.load_sem.at[index])
+        for index in range(2)
+    ]
     heads_load = pltpu.make_async_copy(r.heads_in, r.heads, r.plain_sem.at[2])
-    for copy in sum(loads, plain_loads + [heads_load]):
+    for copy in plain_loads + loads + [heads_load]:
         copy.start()
     stores = []
-    for index, pieces in enumerate(loads):
-        for load in pieces:
-            load.wait()
+    for load, (_, stage, target) in zip(plain_loads, plain):
+        load.wait()
+        store = pltpu.make_async_copy(stage, target, r.store_sem.at[len(stores)])
+        store.start()
+        stores.append(store)
+    for index, load in enumerate(loads):
+        load.wait()
         r.wide[index] = r.narrow[index].astype(F32).reshape(width, width)
         store = pltpu.make_async_copy(r.wide.at[index], (r.up, r.down)[index], r.store_sem.at[len(stores)])
         store.start()
@@ -858,11 +869,6 @@
     ]
     for source, target in parts:
         store = pltpu.make_async_copy(source, target, r.store_sem.at[len(stores)])
-        store.start()
-        stores.append(store)
-    for load, (_, stage, target) in zip(plain_loads, plain):
-        load.wait()
-        store = pltpu.make_async_copy(stage, target, r.store_sem.at[len(stores)])
         store.start()
         stores.append(store)
     rows = (
@@ -939,7 +945,7 @@
     )
     if ringed:
         outputs.update(
-            feed_sum=shape((half // 16, count, 2, 2, 16, width), BF),
+            feed_sum=shape((2, count, 2, 1, half, width), BF),
             heads_sum=shape((heads_parts, 2, count // 2, 1, heads_width // count, width), BF),
         )
     else:
@@ -984,20 +990,19 @@
     )
     given = [name if name == "lengths" else name + "_from" for name in inputs]
     if ringed:
-        parts = half // 16
         spots, small = count // 2, heads_width // count
         scratch.update(
-            feed_opening=pltpu.VMEM((parts, 2, 2, 16, width), BF),
+            feed_opening=pltpu.VMEM((2, 2, 1, half, width), BF),
             heads_out=pltpu.VMEM((heads_parts, spots, 1, small, width), BF),
             heads_half=pltpu.VMEM((heads_parts, spots, 1, small, width), BF),
-            feed_landed=pltpu.VMEM((parts, 2, count - 1, 2, 16, width), BF),
+            feed_landed=pltpu.VMEM((2, 2, count - 1, 1, half, width), BF),
             heads_quarter=pltpu.VMEM((heads_parts, spots - 1, 1, small, width), BF),
-            feed_shared=pltpu.VMEM((parts, count, 2, 2, 16, width), BF),
+            feed_shared=pltpu.VMEM((2, count, 2, 1, half, width), BF),
             heads_shared=pltpu.VMEM((heads_parts, 2, spots, 1, small, width), BF),
             pair_send=pltpu.SemaphoreType.DMA((heads_parts, 2 * spots)),
             pair_recv=pltpu.SemaphoreType.DMA((heads_parts, 2 * spots)),
-            ring_send=pltpu.SemaphoreType.DMA((1, 2)),
-            ring_recv=pltpu.SemaphoreType.DMA((1, parts, 2, 2, count - 1)),
+            ring_send=pltpu.SemaphoreType.DMA((2,)),
+            ring_recv=pltpu.SemaphoreType.DMA((2, 2, 2, count - 1)),
             small_out=pltpu.VMEM((levels, 8, width), F32),
             small_in=pltpu.VMEM((levels, 8, width), F32),
             small_send=pltpu.SemaphoreType.DMA((levels,)),
@@ -1056,7 +1061,7 @@
         heads=pltpu.VMEM(outs[4].shape, BF),
         wide=pltpu.VMEM((3, width, width), F32),
         plain_sem=pltpu.SemaphoreType.DMA((3,)),
-        load_sem=pltpu.SemaphoreType.DMA((2, half // 16)),
+        load_sem=pltpu.SemaphoreType.DMA((2,)),
         store_sem=pltpu.SemaphoreType.DMA((8,)),
         layer_stage=pltpu.VMEM(frames.shape, BF),
         input_stage=pltpu.VMEM(frames.shape, F32),

time: 196 us -> 193 us (0.985)
  Pallas kernels: 195 us -> 192 us
    pallas_call x1, Pallas kernels: 188 us -> 185 us  [shards(): pl.pallas_call(functools.partial(layer, count if ringed else 0, [*given,...]
where the time goes in v3:
time: 193 us
  Pallas kernels  192 us (99%)
    pallas_call x1, Pallas kernels, shards(): pl.pallas_call(functools.partial(layer, count if ringed else 0, [*given,...  185 us
    pallas_call x1, Pallas kernels, shards(): pl.pallas_call(functools.partial(widen, 2 * lanes, [*given, *results, *bu...  6.59 us

profile of v3, /device:TPU:0, one launch (start us, length us, event | category | flops | bytes accessed | tf_op | source)
XLA Modules:
  0.0 192.8 jit_solution(17010995659055991762)
XLA Ops:
  0.7 185.3 %layer.1 = (bf16[2,200,768]{2,1,0:T(8,128)(2,1)}, f32[2,200,768]{2,1,0:T(8,128)}, f32[8,768]{1,0:T(8,128)}, bf16[2,8,2,1,48,768]{5,4,3,2,1,0:T(8,128)(2,1)}, bf16[4,2,4,1,24,768]{5,4,3,2,1,0:T(8,128)(2,1)}) custom-call(s32[2]{0:T(128)} %refs_0_.1, bf16[2,200,768]{2,1,0:T(8,128)(2,1)} %refs_1_.1, f32[2,200,768]{2,1,0:T(8,128)} %refs_2_.1, ...), custom_call_target="tpu_custom_call" | custom-call | tf_op jit(solution)/shard_map/layer/pallas_call | solution.py:1011
  186.0 6.6 %widen.1 = (bf16[2,200,768]{2,1,0:T(8,128)(2,1)}, f32[2,200,768]{2,1,0:T(8,128)}, f32[192,768]{1,0:T(8,128)}, f32[192]{0:T(256)}, f32[192,768]{1,0:T(8,128)}, /*...) custom-call(bf16[2,200,768]{2,1,0:T(8,128)(2,1)} %get-tuple-element., ...), custom_call_target="tpu_custom_call" | custom-call | tf_op jit(solution)/shard_map/widen/pallas_call | solution.py:1069

commit v4 on v3

--- a/solution.py
+++ b/solution.py
@@ -15,9 +15,9 @@
 INVERSE_ROOT_TAU = 0.3989422804014327
 MASKED = -1e30
 VMEM_BYTES = 62 << 20
-POLLS = (1, 1, 0, 1, 1, 1, 1, 1)
+POLLS = (1, 2, 0, 1, 1, 1, 1, 1)
 TAIL = (
-    (1, 1), (0, 3), (2, 1), (1, 2), (3, 1), (2, 2), (1, 3), (3, 2), (2, 3), (3, 3),
+    (1, 1), (2, 1), (0, 3), (1, 2), (3, 1), (2, 2), (3, 2), (1, 3), (2, 3), (3, 3),
 )
 BF = jnp.bfloat16
 F32 = jnp.float32
@@ -781,9 +781,13 @@
         ]
         level = 2
         last = len(pairs) + 1
+        sent = []
         for at, (part, phase) in enumerate(TAIL):
             pieces[part].act(phase)
             poll(POLLS[6])
+            if not queue and not sent:
+                copies[0].start()
+                sent.append(1)
             if at == 1:
                 store_input(seqs - 1)
             if at % 2 == 1 and level <= last:
@@ -794,10 +798,11 @@
                 else:
                     r.sums[...] = rows_total
         poll(len(queue))
+        if not sent:
+            copies[0].start()
         for piece in pieces:
             piece.act(4)
-        for copy in copies:
-            copy.start()
+        copies[1].start()
         rings[0].wait_sends(r.feed_landed)
     else:
         store_input(seqs - 1)

time: 193 us -> 192 us (level)
  no operation moved by 1% of the time
where the time goes in v4:
time: 192 us
  Pallas kernels  191 us (99%)
    pallas_call x1, Pallas kernels, shards(): pl.pallas_call(functools.partial(layer, count if ringed else 0, [*given,...  185 us
    pallas_call x1, Pallas kernels, shards(): pl.pallas_call(functools.partial(widen, 2 * lanes, [*given, *results, *bu...  6.59 us

profile of v4, /device:TPU:0, one launch (start us, length us, event | category | flops | bytes accessed | tf_op | source)
XLA Modules:
  0.0 192.1 jit_solution(10266179599376850383)
XLA Ops:
  0.7 184.6 %layer.1 = (bf16[2,200,768]{2,1,0:T(8,128)(2,1)}, f32[2,200,768]{2,1,0:T(8,128)}, f32[8,768]{1,0:T(8,128)}, bf16[2,8,2,1,48,768]{5,4,3,2,1,0:T(8,128)(2,1)}, bf16[4,2,4,1,24,768]{5,4,3,2,1,0:T(8,128)(2,1)}) custom-call(s32[2]{0:T(128)} %refs_0_.1, bf16[2,200,768]{2,1,0:T(8,128)(2,1)} %refs_1_.1, f32[2,200,768]{2,1,0:T(8,128)} %refs_2_.1, ...), custom_call_target="tpu_custom_call" | custom-call | tf_op jit(solution)/shard_map/layer/pallas_call | solution.py:1016
  185.3 6.6 %widen.1 = (bf16[2,200,768]{2,1,0:T(8,128)(2,1)}, f32[2,200,768]{2,1,0:T(8,128)}, f32[192,768]{1,0:T(8,128)}, f32[192]{0:T(256)}, f32[192,768]{1,0:T(8,128)}, /*...) custom-call(bf16[2,200,768]{2,1,0:T(8,128)(2,1)} %get-tuple-element., ...), custom_call_target="tpu_custom_call" | custom-call | tf_op jit(solution)/shard_map/widen/pallas_call | solution.py:1074

commit v5 on v4

--- a/solution.py
+++ b/solution.py
@@ -773,11 +773,11 @@
     if count:
         place = lax.broadcasted_iota(jnp.int32, r.rows_sum.shape, 0)
         totals.begin(2, jnp.where(place == 7, r.rows_sum[...], totals.end(1)))
-        copies = [
-            pltpu.make_async_copy(shared, out, r.out_sem.at[index, 0])
-            for index, (shared, out) in enumerate(
-                ((r.feed_shared, r.feed_sum), (r.heads_shared, r.heads_sum))
+        copies = [pltpu.make_async_copy(r.feed_shared, r.feed_sum, r.out_sem.at[0, 0])] + [
+            pltpu.make_async_copy(
+                r.heads_shared.at[part], r.heads_sum.at[part], r.piece_sem.at[part]
             )
+            for part in range(1 + heads)
         ]
         level = 2
         last = len(pairs) + 1
@@ -800,9 +800,9 @@
         poll(len(queue))
         if not sent:
             copies[0].start()
-        for piece in pieces:
+        for index, piece in enumerate(pieces):
             piece.act(4)
-        copies[1].start()
+            copies[1 + index].start()
         rings[0].wait_sends(r.feed_landed)
     else:
         store_input(seqs - 1)
@@ -1005,6 +1005,7 @@
             feed_shared=pltpu.VMEM((2, count, 2, 1, half, width), BF),
             heads_shared=pltpu.VMEM((heads_parts, 2, spots, 1, small, width), BF),
             pair_send=pltpu.SemaphoreType.DMA((heads_parts, 2 * spots)),
+            piece_sem=pltpu.SemaphoreType.DMA((heads_parts,)),
             pair_recv=pltpu.SemaphoreType.DMA((heads_parts, 2 * spots)),
             ring_send=pltpu.SemaphoreType.DMA((2,)),
             ring_recv=pltpu.SemaphoreType.DMA((2, 2, 2, count - 1)),

time: 192 us -> 192 us (level)
  no operation moved by 1% of the time
where the time goes in v5:
time: 192 us
  Pallas kernels  191 us (99%)
    pallas_call x1, Pallas kernels, shards(): pl.pallas_call(functools.partial(layer, count if ringed else 0, [*given,...  184 us
    pallas_call x1, Pallas kernels, shards(): pl.pallas_call(functools.partial(widen, 2 * lanes, [*given, *results, *bu...  6.59 us

profile of v5, /device:TPU:0, one launch (start us, length us, event | category | flops | bytes accessed | tf_op | source)
XLA Modules:
  0.0 191.8 jit_solution(16845904544860592470)
XLA Ops:
  0.7 184.4 %layer.1 = (bf16[2,200,768]{2,1,0:T(8,128)(2,1)}, f32[2,200,768]{2,1,0:T(8,128)}, f32[8,768]{1,0:T(8,128)}, bf16[2,8,2,1,48,768]{5,4,3,2,1,0:T(8,128)(2,1)}, bf16[4,2,4,1,24,768]{5,4,3,2,1,0:T(8,128)(2,1)}) custom-call(s32[2]{0:T(128)} %refs_0_.1, bf16[2,200,768]{2,1,0:T(8,128)(2,1)} %refs_1_.1, f32[2,200,768]{2,1,0:T(8,128)} %refs_2_.1, ...), custom_call_target="tpu_custom_call" | custom-call | tf_op jit(solution)/shard_map/layer/pallas_call | solution.py:1017
  185.0 6.6 %widen.1 = (bf16[2,200,768]{2,1,0:T(8,128)(2,1)}, f32[2,200,768]{2,1,0:T(8,128)}, f32[192,768]{1,0:T(8,128)}, f32[192]{0:T(256)}, f32[192,768]{1,0:T(8,128)}, /*...) custom-call(bf16[2,200,768]{2,1,0:T(8,128)(2,1)} %get-tuple-element., ...), custom_call_target="tpu_custom_call" | custom-call | tf_op jit(solution)/shard_map/widen/pallas_call | solution.py:1075
